TPU v7x, 128 devices: a whole 4x4x4 slice. The times are simulated.
128 devices in a mesh: group: 2 (over z_lo), shard: 32 (over x, y, core), tensor: 2 (over z_hi).
Axes of the slice: x: 4, y: 4, z: 4 (z_hi: 2, z_lo: 2; z = z_hi * 2 + z_lo), core: 2. Of those that a mesh axis runs over, the one named last changes fastest.
Arguments:
- down_anchor: float32 [8192, 4096], P('shard', 'tensor'), may hold values from -6 to 6
- down_local: float32 [2, 8192, 4096], P('group', 'shard', 'tensor'), may hold values from -6 to 6
- down_moment: float32 [8192, 4096], P(('shard', 'group'), 'tensor'), may hold values from -4 to 4
- norm_anchor: float32 [2, 4096], P(None, ('shard', 'tensor')), may hold values from 0.5 to 1.5
- norm_local: float32 [2, 2, 4096], P('group', None, ('shard', 'tensor')), may hold values from 0.1 to 1.9
- norm_moment: float32 [2, 4096], P('group', ('shard', 'tensor')), may hold values from -4 to 4
- gate_anchor: float32 [8192, 4096], P('tensor', 'shard'), may hold values from -6 to 6
- gate_local: float32 [2, 8192, 4096], P('group', 'tensor', 'shard'), may hold values from -6 to 6
- gate_moment: float32 [8192, 4096], P('tensor', 'shard'), may hold values from -4 to 4
- factor_basis: float32 [64, 4096], P(None, 'shard'), may hold values from -0.09375 to 0.09375
Outputs:
- new_down_anchor: float32 [8192, 4096], P('shard', 'tensor')
- new_down_moment: float32 [8192, 4096], P(('shard', 'group'), 'tensor')
- new_norm_anchor: float32 [2, 4096], P(None, ('shard', 'tensor'))
- new_norm_moment: float32 [2, 4096], P('group', ('shard', 'tensor'))
- new_gate_anchor: float32 [8192, 4096], P('tensor', 'shard')
- new_gate_moment: float32 [8192, 4096], P('tensor', 'shard')
All inputs are finite; a program needn't handle non-finite values.
Results may differ from a plain program's by a relative error of at most 0.000096.
Values sent between devices are 32-bit elements; how exact they have to be, the bound alone decides.
A program may use at most 64 MiB of HBM per device.

v0:
```python
import jax
from jax import lax
from jax.sharding import PartitionSpec as P

outer_rate = 0.7
momentum = 0.9


def advance(anchor, moment, delta):
    moment_next = momentum * moment + delta
    anchor_next = anchor - outer_rate * (delta + momentum * moment_next)
    return (anchor_next, moment_next)


def rebuild(factors, factor_basis):
    return lax.dot_general(
        factors, factor_basis, (((0,), (0,)), ((), ())), precision=lax.Precision.HIGHEST
    )


def body(
    down_anchor,
    down_local,
    down_moment,
    norm_anchor,
    norm_local,
    norm_moment,
    gate_anchor,
    gate_local,
    gate_moment,
    factor_basis,
):
    groups = lax.axis_size("group")
    group_index = lax.axis_index("group")
    down_diff = down_anchor - down_local[0]
    norm_diff = norm_anchor - norm_local[0]
    gate_diff = gate_anchor - gate_local[0]
    partial_factors = lax.dot_general(
        factor_basis, gate_diff, (((1,), (1,)), ((), ())), precision=lax.Precision.HIGHEST
    )
    down_sum, norm_sum = (
        lax.psum_scatter(down_diff, "group", scatter_dimension=0, tiled=True),
        lax.psum_scatter(norm_diff, "group", scatter_dimension=0, tiled=True),
    )
    factors = lax.psum(partial_factors, ("group", "shard")) / groups
    half_rows = down_sum.shape[0]
    norm_rows = norm_sum.shape[0]
    down_piece = lax.dynamic_slice_in_dim(down_anchor, group_index * half_rows, half_rows, 0)
    norm_piece = lax.dynamic_slice_in_dim(norm_anchor, group_index * norm_rows, norm_rows, 0)
    down_next, new_down_moment = advance(down_piece, down_moment, down_sum / groups)
    norm_next, new_norm_moment = advance(norm_piece, norm_moment, norm_sum / groups)
    new_down_anchor, new_norm_anchor = (
        lax.all_gather(down_next, "group", axis=0, tiled=True),
        lax.all_gather(norm_next, "group", axis=0, tiled=True),
    )
    gate_delta = rebuild(factors, factor_basis)
    new_gate_anchor, new_gate_moment = advance(gate_anchor, gate_moment, gate_delta)
    return (
        new_down_anchor,
        new_down_moment,
        new_norm_anchor,
        new_norm_moment,
        new_gate_anchor,
        new_gate_moment,
    )


def solution(mesh):
    placed = (
        P("shard", "tensor"),
        P("group", "shard", "tensor"),
        P(("shard", "group"), "tensor"),
        P(None, ("shard", "tensor")),
        P("group", None, ("shard", "tensor")),
        P("group", ("shard", "tensor")),
        P("tensor", "shard"),
        P("group", "tensor", "shard"),
        P("tensor", "shard"),
        P(None, "shard"),
    )
    return jax.shard_map(
        body,
        mesh=mesh,
        in_specs=placed,
        out_specs=(
            P("shard", "tensor"),
            P(("shard", "group"), "tensor"),
            P(None, ("shard", "tensor")),
            P("group", ("shard", "tensor")),
            P("tensor", "shard"),
            P("tensor", "shard"),
        ),
        check_vma=False,
    )
```

profile of v0, /device:TPU:1, one launch (start us, length us, event | category | flops | bytes accessed | tf_op | source)
XLA Modules:
  0.0 590.0 jit_solution(18153728079663768907)
XLA Ops:
  8.0 0.0 copy-start
  8.0 0.0 reduce-scatter.2.cloned.1.call-start
  8.1 3.9 bitcast_subtract_fusion.2
  11.9 0.0 copy-start.1
  11.9 0.0 reduce-scatter.2.cloned.1.call-update
  12.0 0.0 all-reduce.3.cloned.1.call-start
  12.0 0.0 copy-done
  12.0 1.5 copy-done.1
  13.5 4.7 convolution_bitcast_fusion
  18.2 0.0 copy-start.2
  18.2 0.0 all-reduce.3.cloned.1.call-update
  18.3 0.0 all-gather.3.cloned.1.call-start
  18.3 0.0 copy-start.6
  18.3 0.0 copy-start.3
  18.3 0.0 copy-start.4
  18.3 0.0 copy-start.5
  18.4 32.1 %reduce-scatter.2.cloned.1.call-done = f32[128,2048]{1,0:T(8,128)} async-done(((f32[256,2048]{1,0:T(8,128)}), f32[128,2048]{1,0:T(8,128)}) %reduce-scatter.2.cloned.1.call-update) | async-done | bytes 1048592 | tf_op jit(solution)/shard_map/reduce_scatter | solution.py:42
  50.5 0.0 copy-done.2
  50.5 3.2 multiply_subtract_fusion.1
  53.7 0.0 all-gather.3.cloned.1.call-update
  53.7 0.0 copy-done.6
  53.7 0.6 dynamic-slice
  54.3 0.0 copy-done.3
  54.3 0.0 copy-done.4
  54.3 3.8 all-reduce
  58.1 0.0 copy-done.5
  58.1 1.2 subtract_bitcast_fusion
  59.3 3.5 all-gather
  62.7 509.9 %all-reduce.3.cloned.1.call-done = f32[64,4096]{0,1:T(8,128)} async-done(((f32[64,4096]{0,1:T(8,128)}), f32[64,4096]{0,1:T(8,128)}) %all-reduce.3.cloned.1.call-update) | async-done | bytes 1048592 | tf_op jit(solution)/shard_map/psum | solution.py:45
  572.6 6.2 %multiply_subtract_fusion = (f32[4096,128]{1,0:T(8,128)}, f32[4096,128]{1,0:T(8,128)}) fusion(f32[4096,128]{1,0:T(8,128)S(1)} %copy-done.1, f32[4096,128]{1,0:T(8,128)} %param.18, f32[64,128]{1,0:T(8,128)S(1)} %copy-done, f32[64,4096]{0,1:T(8,128)} %all-reduce.3.cloned.1.call-done), kind=kOutput, calls=%fused_computation.3 | convolution fusion | flops 406061056 | bytes 9469952 | tf_op jit(solution)/shard_map/dot_general | solution.py:16
  578.9 3.1 copy.19
  582.0 0.6 copy.20
  (2 shorter events, 0.0 us)
Async XLA Ops:
  8.0 4.0 copy-start
  8.0 42.5 %reduce-scatter.2.cloned.1.call-start = ((), (), s32[]{:S(2)}) async-start(), calls=%async_computation.1 | async-start | bytes 3145728 | tf_op jit(solution)/shard_map/reduce_scatter | solution.py:42
  11.9 1.6 copy-start.1
  12.0 560.7 %all-reduce.3.cloned.1.call-start = ((), (), s32[]{:S(2)}) async-start(), calls=%async_computation.3 | async-start | bytes 4194304 | tf_op jit(solution)/shard_map/psum | solution.py:45
  18.2 32.2 %copy-start.2 = (f32[128,2048]{1,0:T(8,128)S(1)}, f32[128,2048]{1,0:T(8,128)}, u32[]{:S(2)}) copy-start(f32[128,2048]{1,0:T(8,128)} %param.12) | copy-start | bytes 3145732
  18.3 560.6 %all-gather.3.cloned.1.call-start = ((), (), s32[]{:S(2)}) async-start(), calls=%async_computation.2 | async-start | bytes 3145728 | tf_op jit(solution)/shard_map/all_gather | solution.py:53
  18.3 35.4 %copy-start.6 = (u32[128]{0:T(128)S(1)}, u32[128]{0:T(128)}, u32[]{:S(2)}) copy-start(u32[128]{0:T(128)} %constant.35) | copy-start | bytes 1540
  18.3 36.0 %copy-start.3 = (f32[2,64]{1,0:T(2,128)S(1)}, f32[2,64]{1,0:T(2,128)}, u32[]{:S(2)}) copy-start(f32[2,64]{1,0:T(2,128)} %param.13) | copy-start | bytes 1540
  18.3 36.0 %copy-start.4 = (f32[1,2,64]{2,1,0:T(2,128)S(1)}, f32[1,2,64]{2,1,0:T(2,128)}, u32[]{:S(2)}) copy-start(f32[1,2,64]{2,1,0:T(2,128)} %param.14) | copy-start | bytes 1540
  18.3 39.8 %copy-start.5 = (f32[1,64]{1,0:T(1,128)S(1)}, f32[1,64]{1,0:T(1,128)}, u32[]{:S(2)}) copy-start(f32[1,64]{1,0:T(1,128)} %param.15) | copy-start | bytes 772
Sparse Core Ops, SparseCore 0:
  12.1 38.3 reduce-scatter.1
  53.8 37.0 all-gather.2
Sparse Core Ops, SparseCore 1:
  18.3 554.3 all-reduce.2
where the time goes:
time: 590 us
  waiting for transfers between devices  542 us (92%)
  between operations  15.6 us (3%)
  matrix products  10.9 us (2%)
  other arithmetic  8.27 us (1%)
  blocking collectives  7.25 us (1%)
    psum x1, waiting for transfers between devices, body(): factors = lax.psum(partial_factors, ('group', 'shard')) / groups  510 us
    reduce_scatter x1, waiting for transfers between devices, body(): lax.psum_scatter(down_diff, 'group', scatter_dimension=0, tiled=True)  32.1 us
  transfers between devices with their start and end apart: 3, of which 2 were waited for; matrix products, arithmetic and copies ran while one was open for 3% of the time, Pallas kernels for 0%

commit v1 on v0

v1 whole, which is shorter than its diff:
```python
import jax
import jax.numpy as jnp
from jax import lax
from jax.experimental import pallas as pl
from jax.experimental.pallas import tpu as pltpu
from jax.sharding import PartitionSpec as P

outer_rate = 0.7
momentum = 0.9
groups = 2

local_weight = outer_rate * (1.0 + momentum) / groups
moment_weight = outer_rate * momentum * momentum
anchor_weight = 1.0 - outer_rate * (1.0 + momentum)

SIDE = 4
HIGHEST = lax.Precision.HIGHEST
MESH = pl.DeviceIdType.MESH


def kernel(
    down_anchor,
    down_local,
    down_moment,
    norm_anchor,
    norm_local,
    norm_moment,
    gate_anchor,
    gate_local,
    gate_moment,
    factor_basis,
    new_down_anchor,
    new_down_moment,
    new_norm_anchor,
    new_norm_moment,
    new_gate_anchor,
    new_gate_moment,
    da,
    dl,
    dm,
    part,
    peer_local,
    peer_part,
    nl,
    nm,
    ga,
    gl,
    gm,
    basis,
    away,
    home,
    from_core,
    from_x,
    row,
    from_y,
    piece,
    from_z,
    whole,
    load_sem,
    store_sem,
    down_send,
    down_recv,
    part_send,
    part_recv,
    norm_send,
    norm_recv,
    core_send,
    core_recv,
    x_send,
    x_recv,
    y_send,
    y_recv,
    z_send,
    z_recv,
):
    g = lax.axis_index("group")
    s = lax.axis_index("shard")
    x, y, core = s // (2 * SIDE), (s // 2) % SIDE, s % 2
    half = da.shape[0] // 2
    wide = gl.shape[0] // 2
    span = wide // SIDE
    tall = piece.shape[0]
    chunks = part_send.shape[0]
    step = half // chunks

    other_group = {"group": 1 - g}
    other_core = {"shard": s + 1 - 2 * core}

    def along_x(d):
        return {"shard": ((x + d) % SIDE) * 2 * SIDE + y * 2 + core}

    def along_y(d):
        return {"shard": x * 2 * SIDE + ((y + d) % SIDE) * 2 + core}

    def remote(src, dst, send, recv, device):
        return pltpu.make_async_remote_copy(
            src_ref=src, dst_ref=dst, send_sem=send, recv_sem=recv, device_id=device, device_id_type=MESH
        )

    barrier = pltpu.get_barrier_semaphore()
    partners = [other_group, other_core]
    partners += [along_x(d) for d in range(1, SIDE)] + [along_y(d) for d in range(1, SIDE)]
    for device in partners:
        pl.semaphore_signal(barrier, inc=1, device_id=device, device_id_type=MESH)

    mine = pl.ds(pl.multiple_of(g * half, half), half)
    theirs = pl.ds(pl.multiple_of((1 - g) * half, half), half)
    near = pl.ds(pl.multiple_of(core * wide, wide), wide)
    far = pl.ds(pl.multiple_of((1 - core) * wide, wide), wide)

    pairs = [
        (factor_basis, basis),
        (gate_anchor.at[far], ga.at[far]),
        (gate_local.at[0, far], gl.at[far]),
        (gate_anchor.at[near], ga.at[near]),
        (gate_local.at[0, near], gl.at[near]),
        (down_local.at[0, mine], dl.at[mine]),
        (down_moment, dm),
        (gate_moment, gm),
        (down_anchor, da),
        (down_local.at[0, theirs], dl.at[theirs]),
    ]
    loads = [pltpu.make_async_copy(src, dst, load_sem.at[i]) for i, (src, dst) in enumerate(pairs)]
    for load in loads:
        load.start()

    pl.semaphore_wait(barrier, len(partners))

    norm_copies = [
        remote(norm_local, nl, norm_send.at[0], norm_recv.at[0], other_group),
        remote(norm_moment, nm, norm_send.at[1], norm_recv.at[1], other_group),
    ]
    for copy in norm_copies:
        copy.start()
    local_copy = remote(down_local.at[0, theirs], peer_local, down_send, down_recv, other_group)
    local_copy.start()

    def factor(start, out):
        def block(i, carry):
            rows = pl.ds(pl.multiple_of(start + i * span, span), span)
            diff = ga[rows, :] - gl[rows, :]
            out[i] = lax.dot_general(
                basis[...], diff, (((1,), (1,)), ((), ())), precision=HIGHEST, preferred_element_type=jnp.float32
            )
            return carry

        lax.fori_loop(0, SIDE, block, 0)

    for load in loads[:3]:
        load.wait()
    factor((1 - core) * wide, away)
    core_copy = remote(away, from_core, core_send.at[0], core_recv.at[0], other_core)
    core_copy.start()
    for load in loads[3:5]:
        load.wait()
    factor(core * wide, home)

    for load in loads[5:7]:
        load.wait()

    def combine(i, carry):
        rows = pl.ds(pl.multiple_of(i * 16, 16), 16)
        own = pl.ds(pl.multiple_of(g * half + i * 16, 16), 16)
        part[rows, :] = local_weight * dl[own, :] - moment_weight * dm[rows, :]
        return carry

    lax.fori_loop(0, half // 16, combine, 0)

    core_copy.wait_recv()
    x_copies = []
    for d in (2, 1, 3):
        to = (x + d) % SIDE
        home[to] = home[to] + from_core[to]
        x_copies.append(remote(home.at[to], from_x.at[d - 1], x_send.at[d - 1], x_recv.at[d - 1], along_x(d)))
        x_copies[-1].start()
    row[...] = home[x] + from_core[x]
    for copy in x_copies:
        copy.wait_recv()
    row[...] = (row[...] + from_x[0]) + (from_x[1] + from_x[2])

    y_copies = []
    for d in (2, 1, 3):
        rows = pl.ds(pl.multiple_of(((y + d) % SIDE) * tall, tall), tall)
        y_copies.append(remote(row.at[rows], from_y.at[d - 1], y_send.at[d - 1], y_recv.at[d - 1], along_y(d)))
        y_copies[-1].start()
    kept = pl.ds(pl.multiple_of(y * tall, tall), tall)
    for copy in y_copies:
        copy.wait_recv()
    piece[...] = (row[kept, :] + from_y[0]) + (from_y[1] + from_y[2])

    z_copy = remote(piece, from_z, z_send, z_recv, other_group)
    z_copy.start()
    part_copies = []
    for i in range(chunks):
        rows = pl.ds(i * step, step)
        part_copies.append(
            remote(part.at[rows], peer_part.at[rows], part_send.at[i], part_recv.at[i], other_group)
        )
        part_copies[-1].start()
    z_copy.wait_recv()

    slot = core * SIDE + x
    whole[slot, kept, :] = (piece[...] + from_z[...]) * (1.0 / groups)
    y_back = []
    for d in (2, 1, 3):
        here = whole.at[slot, kept]
        y_back.append(remote(here, here, y_send.at[d + 2], y_recv.at[d + 2], along_y(d)))
        y_back[-1].start()
    for copy in y_back:
        copy.wait_recv()
    x_back = []
    for d in (2, 1, 3):
        here = whole.at[slot]
        x_back.append(remote(here, here, x_send.at[d + 2], x_recv.at[d + 2], along_x(d)))
        x_back[-1].start()
    for copy in x_back:
        copy.wait_recv()
    ours = whole.at[pl.ds(pl.multiple_of(core * SIDE, SIDE), SIDE)]
    core_back = remote(ours, ours, core_send.at[1], core_recv.at[1], other_core)
    core_back.start()

    loads[7].wait()

    def rebuild(first):
        def block(i, carry):
            rows = pl.ds(pl.multiple_of((first + i) * span, span), span)
            delta = lax.dot_general(
                whole[first + i], basis[...], (((0,), (0,)), ((), ())), precision=HIGHEST,
                preferred_element_type=jnp.float32,
            )
            moment = momentum * gm[rows, :] + delta
            gm[rows, :] = moment
            ga[rows, :] = ga[rows, :] - outer_rate * (delta + momentum * moment)
            return carry

        lax.fori_loop(0, SIDE, block, 0)

    rebuild(core * SIDE)
    core_back.wait_recv()
    rebuild((1 - core) * SIDE)
    stores = [
        pltpu.make_async_copy(ga, new_gate_anchor, store_sem.at[0]),
        pltpu.make_async_copy(gm, new_gate_moment, store_sem.at[1]),
    ]
    for store in stores:
        store.start()

    for copy in norm_copies:
        copy.wait_recv()
    norm_delta = norm_anchor[...] - (norm_local[0] + nl[0]) * (1.0 / groups)
    picked = lax.broadcasted_iota(jnp.int32, norm_anchor.shape, 0) == g
    norm_next = momentum * jnp.where(picked, norm_moment[...], nm[...]) + norm_delta
    new_norm_anchor[...] = norm_anchor[...] - outer_rate * (norm_delta + momentum * norm_next)
    new_norm_moment[...] = jnp.where(g == 0, norm_next[0:1], norm_next[1:2])

    loads[8].wait()
    local_copy.wait_recv()

    def own_half(i, carry):
        rows = pl.ds(pl.multiple_of(i * 16, 16), 16)
        own = pl.ds(pl.multiple_of(g * half + i * 16, 16), 16)
        anchor = da[own, :]
        dm[rows, :] = momentum * dm[rows, :] + (anchor - (dl[own, :] + peer_local[rows, :]) * (1.0 / groups))
        da[own, :] = (anchor_weight * anchor + local_weight * peer_local[rows, :]) + part[rows, :]
        return carry

    lax.fori_loop(0, half // 16, own_half, 0)
    stores += [
        pltpu.make_async_copy(dm, new_down_moment, store_sem.at[2]),
        pltpu.make_async_copy(da.at[mine], new_down_anchor.at[mine], store_sem.at[3]),
    ]
    stores[2].start()
    stores[3].start()
    loads[9].wait()

    for c in range(chunks):
        part_copies[c].wait_recv()

        def other_half(i, carry):
            rows = pl.ds(pl.multiple_of(c * step + i * 8, 8), 8)
            far_rows = pl.ds(pl.multiple_of((1 - g) * half + c * step + i * 8, 8), 8)
            da[far_rows, :] = (
                anchor_weight * da[far_rows, :] + local_weight * dl[far_rows, :]
            ) + peer_part[rows, :]
            return carry

        lax.fori_loop(0, step // 8, other_half, 0)
        chunk = pl.ds(pl.multiple_of((1 - g) * half + c * step, step), step)
        stores.append(pltpu.make_async_copy(da.at[chunk], new_down_anchor.at[chunk], store_sem.at[4 + c]))
        stores[-1].start()

    for copy in norm_copies + [local_copy, core_copy, z_copy, core_back]:
        copy.wait_send()
    for copy in x_copies + y_copies + part_copies + y_back + x_back:
        copy.wait_send()
    for store in stores:
        store.wait()


def body(*args):
    down_anchor, _, down_moment, norm_anchor, norm_local, norm_moment, gate_anchor, _, _, factor_basis = args
    f32 = jnp.float32
    half, width = down_moment.shape
    rank, depth = factor_basis.shape
    hidden = gate_anchor.shape[0]
    wide = hidden // 2
    span = wide // SIDE
    tall = rank // SIDE
    chunks = 4
    anywhere = pl.BlockSpec(memory_space=pl.ANY)
    vmem = pl.BlockSpec(memory_space=pltpu.VMEM)
    dma = pltpu.SemaphoreType.DMA
    shapes = [
        pltpu.VMEM((2 * half, width), f32),
        pltpu.VMEM((2 * half, width), f32),
        pltpu.VMEM((half, width), f32),
        pltpu.VMEM((half, width), f32),
        pltpu.VMEM((half, width), f32),
        pltpu.VMEM((half, width), f32),
        pltpu.VMEM(norm_local.shape, f32),
        pltpu.VMEM(norm_moment.shape, f32),
        pltpu.VMEM((hidden, depth), f32),
        pltpu.VMEM((hidden, depth), f32),
        pltpu.VMEM((hidden, depth), f32),
        pltpu.VMEM((rank, depth), f32),
        pltpu.VMEM((SIDE, rank, span), f32),
        pltpu.VMEM((SIDE, rank, span), f32),
        pltpu.VMEM((SIDE, rank, span), f32),
        pltpu.VMEM((SIDE - 1, rank, span), f32),
        pltpu.VMEM((rank, span), f32),
        pltpu.VMEM((SIDE - 1, tall, span), f32),
        pltpu.VMEM((tall, span), f32),
        pltpu.VMEM((tall, span), f32),
        pltpu.VMEM((2 * SIDE, rank, span), f32),
        dma((10,)),
        dma((4 + chunks,)),
        dma,
        dma,
        dma((chunks,)),
        dma((chunks,)),
        dma((2,)),
        dma((2,)),
        dma((2,)),
        dma((2,)),
        dma((6,)),
        dma((6,)),
        dma((6,)),
        dma((6,)),
        dma,
        dma,
    ]
    outs = [
        jax.ShapeDtypeStruct(a.shape, f32)
        for a in (down_anchor, down_moment, norm_anchor, norm_moment, gate_anchor, gate_anchor)
    ]
    return pl.pallas_call(
        kernel,
        out_shape=outs,
        in_specs=[anywhere] * 3 + [vmem] * 3 + [anywhere] * 4,
        out_specs=[anywhere] * 2 + [vmem] * 2 + [anywhere] * 2,
        scratch_shapes=shapes,
        compiler_params=pltpu.CompilerParams(collective_id=0, has_side_effects=True),
    )(*args)


def solution(mesh):
    placed = (
        P("shard", "tensor"),
        P("group", "shard", "tensor"),
        P(("shard", "group"), "tensor"),
        P(None, ("shard", "tensor")),
        P("group", None, ("shard", "tensor")),
        P("group", ("shard", "tensor")),
        P("tensor", "shard"),
        P("group", "tensor", "shard"),
        P("tensor", "shard"),
        P(None, "shard"),
    )
    return jax.shard_map(
        body,
        mesh=mesh,
        in_specs=placed,
        out_specs=(
            P("shard", "tensor"),
            P(("shard", "group"), "tensor"),
            P(None, ("shard", "tensor")),
            P("group", ("shard", "tensor")),
            P("tensor", "shard"),
            P("tensor", "shard"),
        ),
        check_vma=False,
    )
```

time: 590 us -> 63.9 us (0.11)
  waiting for transfers between devices: 542 us -> 0 us
  Pallas kernels: 0 us -> 54 us
  between operations: 15.6 us -> 0.67 us
  matrix products: 10.9 us -> 0 us
  other arithmetic: 8.27 us -> 0 us
  blocking collectives: 7.25 us -> 0 us
    psum x1 -> x0, waiting for transfers between devices: 510 us -> none  [body(): factors = lax.psum(partial_factors, ('group', 'shard')) / groups]
    pallas_call x0 -> x1, Pallas kernels: none -> 54 us  [body(): pl.pallas_call(kernel, out_shape=outs, in_specs=[anywhere] * 3 + [vmem] *...]
    reduce_scatter x1 -> x0, waiting for transfers between devices: 32.1 us -> none  [body(): lax.psum_scatter(down_diff, 'group', scatter_dimension=0, tiled=True)]
    dot_general x2 -> x0, matrix products: 10.9 us -> none  [the longest x1 6.22 us: rebuild(): lax.dot_general(factors, factor_basis, (((0,), (0,)), ((), ())), precisio...]
    sub x3 -> x0, other arithmetic: 7.1 us -> none  [the longest x1 3.88 us: body(): down_diff = down_anchor - down_local[0]]
  transfers between devices with their start and end apart: 3 -> 0, of which waited for: 2 -> 0; matrix products, arithmetic and copies ran while one was open for 3% -> 0% of each run, Pallas kernels for 0% -> 0%
where the time goes in v1:
time: 63.9 us; the launch traced here: 63.6 us
  Pallas kernels  54 us (85%)
  local copies, waits for them, and re-layouts  8.95 us (14%)
  between operations  0.67 us (1%)
    pallas_call x1, Pallas kernels, body(): pl.pallas_call(kernel, out_shape=outs, in_specs=[anywhere] * 3 + [vmem] *...  54 us
    unnamed x16, local copies, waits for them, and re-layouts  8.95 us

profile of v1, /device:TPU:1, one launch (start us, length us, event | category | flops | bytes accessed | tf_op | source)
XLA Modules:
  0.0 63.6 jit_solution(5476648904989923957)
XLA Ops:
  0.6 54.0 %shard_map.145 = (f32[256,2048]{1,0:T(8,128)}, f32[128,2048]{1,0:T(8,128)}, f32[2,64]{1,0:T(2,128)}, f32[1,64]{1,0:T(1,128)}, f32[4096,128]{1,0:T(8,128)}, /*index=5*/f32[4096,128]{1,0:T(8,128)}) custom-call(f32[256,2048]{1,0:T(8,128)} %down_anchor.1, f32[1,256,2048]{2,1,0:T(8,128)} %down_local.1, f32[128,2048]{1,0:T(8,128)} %down_moment.1, ...), custom_call_target="tpu_custom_call" | custom-call | tf_op jit(solution)/shard_map/pallas_call | solution.py:356
  54.7 0.0 copy-start.2
  54.7 0.0 copy-start.3
  54.7 3.2 %copy.22 = f32[256,2048]{1,0:T(8,128)} copy(f32[256,2048]{1,0:T(8,128)} %get-tuple-element.12) | data formatting | bytes 4194304
  57.9 0.0 copy-done.2
  57.9 0.0 copy-start.4
  57.9 0.0 copy-start.1
  57.9 1.0 %copy.23 = f32[128,2048]{1,0:T(8,128)} copy(f32[128,2048]{1,0:T(8,128)S(1)} %copy-done.2) | data formatting | bytes 2097152
  58.9 0.0 copy-done.3
  58.9 0.6 copy.24
  59.4 0.0 copy-done.4
  59.4 0.5 copy.25
  60.0 0.0 copy-done.1
  60.0 0.0 copy-start
  60.0 1.3 %copy.26 = f32[4096,128]{1,0:T(8,128)} copy(f32[4096,128]{1,0:T(8,128)S(1)} %copy-done.1) | data formatting | bytes 4194304
  61.3 1.0 %copy-done = f32[4096,128]{1,0:T(8,128)S(1)} copy-done((f32[4096,128]{1,0:T(8,128)S(1)}, f32[4096,128]{1,0:T(8,128)}, u32[]{:S(2)}) %copy-start) | copy-done | bytes 2097176
  62.3 1.3 %copy.27 = f32[4096,128]{1,0:T(8,128)} copy(f32[4096,128]{1,0:T(8,128)S(1)} %copy-done) | data formatting | bytes 4194304
Async XLA Ops:
  54.7 3.2 %copy-start.2 = (f32[128,2048]{1,0:T(8,128)S(1)}, f32[128,2048]{1,0:T(8,128)}, u32[]{:S(2)}) copy-start(f32[128,2048]{1,0:T(8,128)} %get-tuple-element.13) | copy-start | bytes 3145732
  54.7 4.2 %copy-start.3 = (f32[2,64]{1,0:T(2,128)S(1)}, f32[2,64]{1,0:T(2,128)}, u32[]{:S(2)}) copy-start(f32[2,64]{1,0:T(2,128)} %get-tuple-element.14) | copy-start | bytes 1540
  57.9 1.5 %copy-start.4 = (f32[1,64]{1,0:T(1,128)S(1)}, f32[1,64]{1,0:T(1,128)}, u32[]{:S(2)}) copy-start(f32[1,64]{1,0:T(1,128)} %get-tuple-element.15) | copy-start | bytes 772
  57.9 2.1 %copy-start.1 = (f32[4096,128]{1,0:T(8,128)S(1)}, f32[4096,128]{1,0:T(8,128)}, u32[]{:S(2)}) copy-start(f32[4096,128]{1,0:T(8,128)} %get-tuple-element.16) | copy-start | bytes 6291460
  60.0 2.3 %copy-start = (f32[4096,128]{1,0:T(8,128)S(1)}, f32[4096,128]{1,0:T(8,128)}, u32[]{:S(2)}) copy-start(f32[4096,128]{1,0:T(8,128)} %get-tuple-element.17) | copy-start | bytes 6291460

commit v2 on v1

--- a/solution.py
+++ b/solution.py
@@ -29,23 +29,19 @@
     gate_local,
     gate_moment,
     factor_basis,
-    new_down_anchor,
-    new_down_moment,
+    da,
+    dm,
     new_norm_anchor,
     new_norm_moment,
-    new_gate_anchor,
-    new_gate_moment,
-    da,
+    ga,
+    gm,
     dl,
-    dm,
     part,
     peer_local,
     peer_part,
     nl,
     nm,
-    ga,
     gl,
-    gm,
     basis,
     away,
     home,
@@ -57,7 +53,6 @@
     from_z,
     whole,
     load_sem,
-    store_sem,
     down_send,
     down_recv,
     part_send,
@@ -238,12 +233,6 @@
     rebuild(core * SIDE)
     core_back.wait_recv()
     rebuild((1 - core) * SIDE)
-    stores = [
-        pltpu.make_async_copy(ga, new_gate_anchor, store_sem.at[0]),
-        pltpu.make_async_copy(gm, new_gate_moment, store_sem.at[1]),
-    ]
-    for store in stores:
-        store.start()
 
     for copy in norm_copies:
         copy.wait_recv()
@@ -265,12 +254,6 @@
         return carry
 
     lax.fori_loop(0, half // 16, own_half, 0)
-    stores += [
-        pltpu.make_async_copy(dm, new_down_moment, store_sem.at[2]),
-        pltpu.make_async_copy(da.at[mine], new_down_anchor.at[mine], store_sem.at[3]),
-    ]
-    stores[2].start()
-    stores[3].start()
     loads[9].wait()
 
     for c in range(chunks):
@@ -285,16 +268,23 @@
             return carry
 
         lax.fori_loop(0, step // 8, other_half, 0)
-        chunk = pl.ds(pl.multiple_of((1 - g) * half + c * step, step), step)
-        stores.append(pltpu.make_async_copy(da.at[chunk], new_down_anchor.at[chunk], store_sem.at[4 + c]))
-        stores[-1].start()
 
     for copy in norm_copies + [local_copy, core_copy, z_copy, core_back]:
         copy.wait_send()
     for copy in x_copies + y_copies + part_copies + y_back + x_back:
         copy.wait_send()
-    for store in stores:
-        store.wait()
+
+
+def write_out(*refs):
+    count = len(refs) // 2
+    sems = refs[-1]
+    copies = [pltpu.make_async_copy(refs[i], refs[count + i], sems.at[i]) for i in (0, 1, 4, 5)]
+    for copy in copies:
+        copy.start()
+    for i in (2, 3):
+        refs[count + i][...] = refs[i][...]
+    for copy in copies:
+        copy.wait()
 
 
 def body(*args):
@@ -312,15 +302,11 @@
     dma = pltpu.SemaphoreType.DMA
     shapes = [
         pltpu.VMEM((2 * half, width), f32),
-        pltpu.VMEM((2 * half, width), f32),
-        pltpu.VMEM((half, width), f32),
         pltpu.VMEM((half, width), f32),
         pltpu.VMEM((half, width), f32),
         pltpu.VMEM((half, width), f32),
         pltpu.VMEM(norm_local.shape, f32),
         pltpu.VMEM(norm_moment.shape, f32),
-        pltpu.VMEM((hidden, depth), f32),
-        pltpu.VMEM((hidden, depth), f32),
         pltpu.VMEM((hidden, depth), f32),
         pltpu.VMEM((rank, depth), f32),
         pltpu.VMEM((SIDE, rank, span), f32),
@@ -333,7 +319,6 @@
         pltpu.VMEM((tall, span), f32),
         pltpu.VMEM((2 * SIDE, rank, span), f32),
         dma((10,)),
-        dma((4 + chunks,)),
         dma,
         dma,
         dma((chunks,)),
@@ -349,18 +334,23 @@
         dma,
         dma,
     ]
-    outs = [
-        jax.ShapeDtypeStruct(a.shape, f32)
-        for a in (down_anchor, down_moment, norm_anchor, norm_moment, gate_anchor, gate_anchor)
-    ]
+    held = [pltpu.VMEM(a.shape, f32) for a in (down_anchor, down_moment, norm_anchor, norm_moment, gate_anchor, gate_anchor)]
+    results = pl.pallas_call(
+        kernel,
+        out_shape=held,
+        in_specs=[anywhere] * 3 + [vmem] * 3 + [anywhere] * 4,
+        out_specs=[vmem] * 6,
+        scratch_shapes=shapes,
+        compiler_params=pltpu.CompilerParams(collective_id=0, has_side_effects=True, vmem_limit_bytes=48 << 20),
+    )(*args)
     return pl.pallas_call(
-        kernel,
-        out_shape=outs,
-        in_specs=[anywhere] * 3 + [vmem] * 3 + [anywhere] * 4,
+        write_out,
+        out_shape=[jax.ShapeDtypeStruct(a.shape, f32) for a in held],
+        in_specs=[vmem] * 6,
         out_specs=[anywhere] * 2 + [vmem] * 2 + [anywhere] * 2,
-        scratch_shapes=shapes,
-        compiler_params=pltpu.CompilerParams(collective_id=0, has_side_effects=True),
-    )(*args)
+        scratch_shapes=[dma((6,))],
+        compiler_params=pltpu.CompilerParams(vmem_limit_bytes=8 << 20),
+    )(*results)
 
 
 def solution(mesh):

time: 63.9 us -> 57.3 us (0.90)
  local copies, waits for them, and re-layouts: 8.95 us -> 0 us
  Pallas kernels: 54 us -> 56.4 us
    unnamed x16 -> x0, local copies, waits for them, and re-layouts: 8.95 us -> none
    pallas_call x1 -> x2, Pallas kernels: 54 us -> 56.4 us  [the longest x1 52.7 us: body(): pl.pallas_call(kernel, out_shape=held, in_specs=[anywhere] * 3 + [vmem] *...]
where the time goes in v2:
time: 57.3 us; the launch traced here: 57 us
  Pallas kernels  56.4 us (98%)
  between operations  0.64 us (1%)
    pallas_call x1, Pallas kernels, body(): pl.pallas_call(kernel, out_shape=held, in_specs=[anywhere] * 3 + [vmem] *...  52.7 us
    pallas_call x1, Pallas kernels, body(): pl.pallas_call(write_out, out_shape=[jax.ShapeDtypeStruct(a.shape, f32) f...  3.66 us

profile of v2, /device:TPU:1, one launch (start us, length us, event | category | flops | bytes accessed | tf_op | source)
XLA Modules:
  0.0 57.0 jit_solution(5891994240591340469)
XLA Ops:
  0.6 52.7 %shard_map.145 = (f32[256,2048]{1,0:T(8,128)S(1)}, f32[128,2048]{1,0:T(8,128)S(1)}, f32[2,64]{1,0:T(2,128)S(1)}, f32[1,64]{1,0:T(1,128)S(1)}, f32[4096,128]{1,0:T(8,128)S(1)}, /*index=5*/f32[4096,128]{1,0:T(8,128)S(1)}) custom-call(f32[256,2048]{1,0:T(8,128)} %down_anchor.1, f32[1,256,2048]{2,1,0:T(8,128)} %down_local.1, f32[128,2048]{1,0:T(8,128)} %down_moment.1, ...), custom_call_target="tpu_custom_call" | custom-call | tf_op jit(solution)/shard_map/pallas_call | solution.py:338
  53.4 3.7 %shard_map.146 = (f32[256,2048]{1,0:T(8,128)}, f32[128,2048]{1,0:T(8,128)}, f32[2,64]{1,0:T(2,128)}, f32[1,64]{1,0:T(1,128)}, f32[4096,128]{1,0:T(8,128)}, /*index=5*/f32[4096,128]{1,0:T(8,128)}) custom-call(f32[256,2048]{1,0:T(8,128)S(1)} %get-tuple-element.12.refs_0_, f32[128,2048]{1,0:T(8,128)S(1)} %get-tuple-element.13.refs_1_, ...), custom_call_target="tpu_custom_call" | custom-call | tf_op jit(solution)/shard_map/pallas_call | solution.py:346

commit v3 on v0

v3 whole, which is shorter than its diff:
```python
import jax
import jax.numpy as jnp
from jax import lax
from jax.experimental import pallas as pl
from jax.experimental.pallas import tpu as pltpu
from jax.sharding import PartitionSpec as P

outer_rate = 0.7
momentum = 0.9
groups = 2

local_weight = outer_rate * (1.0 + momentum) / groups
moment_weight = outer_rate * momentum * momentum
anchor_weight = 1.0 - outer_rate * (1.0 + momentum)

SIDE = 4
HIGHEST = lax.Precision.HIGHEST
MESH = pl.DeviceIdType.MESH


def ring(s, axis_x):
    x, y, core = s // (2 * SIDE), (s // 2) % SIDE, s % 2

    def along_x(d):
        return {"shard": ((x + d) % SIDE) * 2 * SIDE + y * 2 + core}

    def along_y(d):
        return {"shard": x * 2 * SIDE + ((y + d) % SIDE) * 2 + core}

    return along_x if axis_x else along_y


def remote(src, dst, send, recv, device):
    return pltpu.make_async_remote_copy(
        src_ref=src, dst_ref=dst, send_sem=send, recv_sem=recv, device_id=device, device_id_type=MESH
    )


def meet(partners):
    barrier = pltpu.get_barrier_semaphore()
    for device in partners:
        pl.semaphore_signal(barrier, inc=1, device_id=device, device_id_type=MESH)
    pl.semaphore_wait(barrier, len(partners))


def take_raw(down_local, raw, sem):
    half = raw.shape[0]
    g = lax.axis_index("group")
    theirs = pl.ds(pl.multiple_of((1 - g) * half, half), half)
    copy = pltpu.make_async_copy(down_local.at[0, theirs], raw, sem)
    copy.start()
    copy.wait()


def combine(down_local, down_moment, raw, part, dl, dm, sem):
    half = part.shape[0]
    g = lax.axis_index("group")
    mine = pl.ds(pl.multiple_of(g * half, half), half)
    loads = [
        pltpu.make_async_copy(down_local.at[0, mine], dl, sem.at[0]),
        pltpu.make_async_copy(down_moment, dm, sem.at[1]),
    ]
    for load in loads:
        load.start()
    for load in loads:
        load.wait()

    def block(i, carry):
        rows = pl.ds(pl.multiple_of(i * 16, 16), 16)
        part[rows, :] = local_weight * dl[rows, :] - moment_weight * dm[rows, :]
        return carry

    lax.fori_loop(0, half // 16, block, 0)


def reduce_factors(
    gate_anchor, gate_local, factor_basis, norm_local, norm_moment, out,
    ga, gl, basis, away, home, from_core, from_x, row, from_y,
    load_sem, core_send, core_recv, x_send, x_recv, y_send, y_recv,
):
    s = lax.axis_index("shard")
    x, y, core = s // (2 * SIDE), (s // 2) % SIDE, s % 2
    along_x, along_y = ring(s, True), ring(s, False)
    other_core = {"shard": s + 1 - 2 * core}
    wide = gl.shape[0] // 2
    span = wide // SIDE
    tall = from_y.shape[1]
    near = pl.ds(pl.multiple_of(core * wide, wide), wide)
    far = pl.ds(pl.multiple_of((1 - core) * wide, wide), wide)
    pairs = [
        (factor_basis, basis),
        (gate_anchor.at[far], ga.at[far]),
        (gate_local.at[0, far], gl.at[far]),
        (gate_anchor.at[near], ga.at[near]),
        (gate_local.at[0, near], gl.at[near]),
    ]
    loads = [pltpu.make_async_copy(src, dst, load_sem.at[i]) for i, (src, dst) in enumerate(pairs)]
    for load in loads:
        load.start()
    meet([other_core] + [along_x(d) for d in range(1, SIDE)] + [along_y(d) for d in range(1, SIDE)])

    def factor(start, target):
        def block(i, carry):
            rows = pl.ds(pl.multiple_of(start + i * span, span), span)
            diff = ga[rows, :] - gl[rows, :]
            target[i] = lax.dot_general(
                basis[...], diff, (((1,), (1,)), ((), ())), precision=HIGHEST, preferred_element_type=jnp.float32
            )
            return carry

        lax.fori_loop(0, SIDE, block, 0)

    for load in loads[:3]:
        load.wait()
    factor((1 - core) * wide, away)
    core_copy = remote(away, from_core, core_send, core_recv, other_core)
    core_copy.start()
    for load in loads[3:5]:
        load.wait()
    factor(core * wide, home)
    out[tall:, :] = jnp.zeros((8, span), jnp.float32)
    out[tall : tall + 2, 0 : norm_local.shape[2]] = norm_local[0]
    out[tall + 2 : tall + 3, 0 : norm_local.shape[2]] = norm_moment[...]
    core_copy.wait_recv()
    x_copies = []
    for d in (2, 1, 3):
        to = (x + d) % SIDE
        home[to] = home[to] + from_core[to]
        x_copies.append(remote(home.at[to], from_x.at[d - 1], x_send.at[d - 1], x_recv.at[d - 1], along_x(d)))
        x_copies[-1].start()
    row[...] = home[x] + from_core[x]
    for copy in x_copies:
        copy.wait_recv()
    row[...] = (row[...] + from_x[0]) + (from_x[1] + from_x[2])
    y_copies = []
    for d in (2, 1, 3):
        rows = pl.ds(pl.multiple_of(((y + d) % SIDE) * tall, tall), tall)
        y_copies.append(remote(row.at[rows], from_y.at[d - 1], y_send.at[d - 1], y_recv.at[d - 1], along_y(d)))
        y_copies[-1].start()
    kept = pl.ds(pl.multiple_of(y * tall, tall), tall)
    for copy in y_copies:
        copy.wait_recv()
    out[0:tall, :] = (row[kept, :] + from_y[0]) + (from_y[1] + from_y[2])
    for copy in [core_copy] + x_copies + y_copies:
        copy.wait_send()


def gather_factors(
    own, peer, norm_anchor, out, new_norm_anchor, new_norm_moment,
    whole, core_send, core_recv, x_send, x_recv, y_send, y_recv,
):
    g = lax.axis_index("group")
    s = lax.axis_index("shard")
    x, y, core = s // (2 * SIDE), (s // 2) % SIDE, s % 2
    along_x, along_y = ring(s, True), ring(s, False)
    other_core = {"shard": s + 1 - 2 * core}
    tall = whole.shape[1] // SIDE
    meet([other_core] + [along_x(d) for d in range(1, SIDE)] + [along_y(d) for d in range(1, SIDE)])
    slot = core * SIDE + x
    kept = pl.ds(pl.multiple_of(y * tall, tall), tall)
    whole[slot, kept, :] = (own[0:tall, :] + peer[0:tall, :]) * (1.0 / groups)
    y_back = []
    for d in (2, 1, 3):
        here = whole.at[slot, kept]
        y_back.append(remote(here, here, y_send.at[d - 1], y_recv.at[d - 1], along_y(d)))
        y_back[-1].start()
    lanes = norm_anchor.shape[1]
    ours = own[tall : tall + 8, 0:lanes]
    theirs = peer[tall : tall + 8, 0:lanes]
    norm_delta = norm_anchor[...] - (ours[0:2] + theirs[0:2]) * (1.0 / groups)
    picked = lax.broadcasted_iota(jnp.int32, norm_anchor.shape, 0) == g
    norm_next = momentum * jnp.where(picked, ours[2:3], theirs[2:3]) + norm_delta
    new_norm_anchor[...] = norm_anchor[...] - outer_rate * (norm_delta + momentum * norm_next)
    new_norm_moment[...] = jnp.where(g == 0, norm_next[0:1], norm_next[1:2])
    for copy in y_back:
        copy.wait_recv()
    x_back = []
    for d in (2, 1, 3):
        here = whole.at[slot]
        x_back.append(remote(here, here, x_send.at[d - 1], x_recv.at[d - 1], along_x(d)))
        x_back[-1].start()
    for copy in x_back:
        copy.wait_recv()
    half = whole.at[pl.ds(pl.multiple_of(core * SIDE, SIDE), SIDE)]
    core_back = remote(half, half, core_send, core_recv, other_core)
    core_back.start()
    core_back.wait_recv()

    def move(i, carry):
        out[i] = whole[i]
        return carry

    lax.fori_loop(0, 2 * SIDE, move, 0)
    for copy in y_back + x_back + [core_back]:
        copy.wait_send()


def rebuild(
    gate_anchor, gate_moment, factor_basis, whole, norm_a, norm_m,
    new_anchor, new_moment, new_norm_anchor, new_norm_moment, ga, gm, load_sem, store_sem,
):
    blocks = whole.shape[0]
    span = whole.shape[2]
    loads, stores = [], []
    for i in range(blocks):
        rows = pl.ds(i * span, span)
        loads.append(pltpu.make_async_copy(gate_anchor.at[rows], ga.at[rows], load_sem.at[2 * i]))
        loads.append(pltpu.make_async_copy(gate_moment.at[rows], gm.at[rows], load_sem.at[2 * i + 1]))
        stores.append(pltpu.make_async_copy(ga.at[rows], new_anchor.at[rows], store_sem.at[2 * i]))
        stores.append(pltpu.make_async_copy(gm.at[rows], new_moment.at[rows], store_sem.at[2 * i + 1]))
    for load in loads:
        load.start()
    new_norm_anchor[...] = norm_a[...]
    new_norm_moment[...] = norm_m[...]
    for i in range(blocks):
        rows = pl.ds(i * span, span)
        delta = lax.dot_general(
            whole[i], factor_basis[...], (((0,), (0,)), ((), ())), precision=HIGHEST,
            preferred_element_type=jnp.float32,
        )
        loads[2 * i].wait()
        loads[2 * i + 1].wait()
        moment = momentum * gm[rows, :] + delta
        gm[rows, :] = moment
        ga[rows, :] = ga[rows, :] - outer_rate * (delta + momentum * moment)
        stores[2 * i].start()
        stores[2 * i + 1].start()
    for store in stores:
        store.wait()


def own_half(
    down_anchor, down_moment, raw, peer, down_local, part,
    new_anchor, new_moment, base, da, dm, dl, pr, load_sem, store_sem,
):
    half = part.shape[0]
    g = lax.axis_index("group")
    mine = pl.ds(pl.multiple_of(g * half, half), half)
    pairs = [
        (down_anchor, da),
        (down_moment, dm),
        (down_local.at[0, mine], dl),
        (peer, pr),
    ]
    loads = [pltpu.make_async_copy(src, dst, load_sem.at[i]) for i, (src, dst) in enumerate(pairs)]
    for load in loads:
        load.start()
    for load in loads:
        load.wait()

    def block(i, carry):
        rows = pl.ds(pl.multiple_of(i * 16, 16), 16)
        own = pl.ds(pl.multiple_of(g * half + i * 16, 16), 16)
        anchor = da[own, :]
        dm[rows, :] = momentum * dm[rows, :] + (anchor - (dl[rows, :] + pr[rows, :]) * (1.0 / groups))
        da[own, :] = (anchor_weight * anchor + local_weight * pr[rows, :]) + part[rows, :]
        far = pl.ds(pl.multiple_of((1 - g) * half + i * 16, 16), 16)
        base[rows, :] = anchor_weight * da[far, :] + local_weight * raw[rows, :]
        return carry

    lax.fori_loop(0, half // 16, block, 0)
    stores = [
        pltpu.make_async_copy(da.at[mine], new_anchor.at[mine], store_sem.at[0]),
        pltpu.make_async_copy(dm, new_moment, store_sem.at[1]),
    ]
    for store in stores:
        store.start()
    for store in stores:
        store.wait()


def other_half(given, base, peer, new_anchor, result, sem):
    del given
    half = base.shape[0]
    chunks = sem.shape[0]
    step = half // chunks
    g = lax.axis_index("group")
    stores = []
    for c in range(chunks):
        def block(i, carry):
            rows = pl.ds(pl.multiple_of(c * step + i * 8, 8), 8)
            result[rows, :] = base[rows, :] + peer[rows, :]
            return carry

        lax.fori_loop(0, step // 8, block, 0)
        rows = pl.ds(c * step, step)
        far = pl.ds(pl.multiple_of((1 - g) * half + c * step, step), step)
        stores.append(pltpu.make_async_copy(result.at[rows], new_anchor.at[far], sem.at[c]))
        stores[-1].start()
    for store in stores:
        store.wait()


def body(*args):
    (down_anchor, down_local, down_moment, norm_anchor, norm_local, norm_moment, gate_anchor, gate_local, gate_moment,
     factor_basis) = args
    f32 = jnp.float32
    half, width = down_moment.shape
    rank, depth = factor_basis.shape
    hidden = gate_anchor.shape[0]
    wide = hidden // 2
    span = wide // SIDE
    tall = rank // SIDE
    anywhere = pl.BlockSpec(memory_space=pl.ANY)
    vmem = pl.BlockSpec(memory_space=pltpu.VMEM)
    dma = pltpu.SemaphoreType.DMA
    V = lambda *shape: pltpu.VMEM(shape, f32)
    S = lambda a: jax.ShapeDtypeStruct(a.shape, f32)
    swap = [(0, 1), (1, 0)]

    def cost(us):
        return pl.CostEstimate(flops=0, bytes_accessed=int(us * 3.5e6), transcendentals=0)

    def params(mib, **more):
        return pltpu.CompilerParams(vmem_limit_bytes=mib << 20, **more)

    raw = pl.pallas_call(
        take_raw, out_shape=V(half, width), in_specs=[pl.BlockSpec(memory_space=pltpu.HBM)], out_specs=vmem, scratch_shapes=[dma],
        compiler_params=params(8), cost_estimate=cost(1),
    )(down_local)
    peer_raw = lax.ppermute(raw, "group", swap)
    part = pl.pallas_call(
        combine, out_shape=V(half, width), in_specs=[anywhere] * 2 + [vmem], out_specs=vmem,
        scratch_shapes=[V(half, width), V(half, width), dma((2,))], compiler_params=params(8), cost_estimate=cost(2),
    )(down_local, down_moment, raw)
    own = pl.pallas_call(
        reduce_factors,
        out_shape=V(tall + 8, span),
        in_specs=[anywhere] * 2 + [vmem] * 3,
        out_specs=vmem,
        scratch_shapes=[
            V(hidden, depth), V(hidden, depth), V(rank, depth), V(SIDE, rank, span), V(SIDE, rank, span),
            V(SIDE, rank, span), V(SIDE - 1, rank, span), V(rank, span), V(SIDE - 1, tall, span),
            dma((5,)), dma, dma, dma((3,)), dma((3,)), dma((3,)), dma((3,)),
        ],
        compiler_params=params(16, collective_id=0, has_side_effects=True), cost_estimate=cost(20),
    )(gate_anchor, gate_local, factor_basis, norm_local, norm_moment)
    peer = lax.ppermute(own, "group", swap)
    peer, part = lax.optimization_barrier((peer, part))
    peer_part = lax.ppermute(part, "group", swap)
    whole, norm_a, norm_m = pl.pallas_call(
        gather_factors,
        out_shape=[V(2 * SIDE, rank, span), V(*norm_anchor.shape), V(*norm_moment.shape)],
        in_specs=[vmem] * 3,
        out_specs=[vmem] * 3,
        scratch_shapes=[V(2 * SIDE, rank, span), dma, dma, dma((3,)), dma((3,)), dma((3,)), dma((3,))],
        compiler_params=params(8, collective_id=1, has_side_effects=True), cost_estimate=cost(15),
    )(own, peer, norm_anchor)
    new_gate_anchor, new_gate_moment, new_norm_anchor, new_norm_moment = pl.pallas_call(
        rebuild,
        out_shape=[S(gate_anchor), S(gate_moment), S(norm_anchor), S(norm_moment)],
        in_specs=[anywhere] * 2 + [vmem] * 4,
        out_specs=[anywhere] * 2 + [vmem] * 2,
        scratch_shapes=[V(hidden, depth), V(hidden, depth), dma((4 * SIDE,)), dma((4 * SIDE,))],
        compiler_params=params(16), cost_estimate=cost(5),
    )(gate_anchor, gate_moment, factor_basis, whole, norm_a, norm_m)
    peer_raw, _ = lax.optimization_barrier((peer_raw, whole))
    anchor, new_down_moment, base = pl.pallas_call(
        own_half,
        out_shape=[S(down_anchor), S(down_moment), V(half, width)],
        in_specs=[anywhere] * 2 + [vmem, anywhere, anywhere, vmem],
        out_specs=[anywhere] * 2 + [vmem],
        scratch_shapes=[V(2 * half, width)] + [V(half, width)] * 3 + [dma((4,)), dma((2,))],
        compiler_params=params(16), cost_estimate=cost(4),
    )(down_anchor, down_moment, raw, peer_raw, down_local, part)
    new_down_anchor = pl.pallas_call(
        other_half,
        out_shape=S(down_anchor),
        in_specs=[anywhere, vmem, vmem],
        out_specs=anywhere,
        input_output_aliases={0: 0},
        scratch_shapes=[V(half, width), dma((4,))],
        compiler_params=params(8), cost_estimate=cost(1),
    )(anchor, base, peer_part)
    return new_down_anchor, new_down_moment, new_norm_anchor, new_norm_moment, new_gate_anchor, new_gate_moment


def solution(mesh):
    placed = (
        P("shard", "tensor"),
        P("group", "shard", "tensor"),
        P(("shard", "group"), "tensor"),
        P(None, ("shard", "tensor")),
        P("group", None, ("shard", "tensor")),
        P("group", ("shard", "tensor")),
        P("tensor", "shard"),
        P("group", "tensor", "shard"),
        P("tensor", "shard"),
        P(None, "shard"),
    )
    return jax.shard_map(
        body,
        mesh=mesh,
        in_specs=placed,
        out_specs=(
            P("shard", "tensor"),
            P(("shard", "group"), "tensor"),
            P(None, ("shard", "tensor")),
            P("group", ("shard", "tensor")),
            P("tensor", "shard"),
            P("tensor", "shard"),
        ),
        check_vma=False,
    )
```

time: 590 us -> 76.4 us (0.13)
  waiting for transfers between devices: 542 us -> 17.8 us
  Pallas kernels: 0 us -> 48.1 us
  between operations: 15.6 us -> 0.78 us
  matrix products: 10.9 us -> 0 us
  other arithmetic: 8.27 us -> 0 us
  blocking collectives: 7.25 us -> 0 us
    psum x1 -> x0, waiting for transfers between devices: 510 us -> none  [body(): factors = lax.psum(partial_factors, ('group', 'shard')) / groups]
    pallas_call x0 -> x7, Pallas kernels: none -> 48.1 us  [the longest x1 20 us: body(): pl.pallas_call(reduce_factors, out_shape=V(tall + 8, span), in_specs=[any...]
    reduce_scatter x1 -> x0, waiting for transfers between devices: 32.1 us -> none  [body(): lax.psum_scatter(down_diff, 'group', scatter_dimension=0, tiled=True)]
    ppermute x0 -> x3, waiting for transfers between devices: none -> 17.8 us  [the longest x1 17 us: body(): peer_part = lax.ppermute(part, 'group', swap)]
    dot_general x2 -> x0, matrix products: 10.9 us -> none  [the longest x1 6.22 us: rebuild(): lax.dot_general(factors, factor_basis, (((0,), (0,)), ((), ())), precisio...]
    sub x3 -> x0, other arithmetic: 7.1 us -> none  [the longest x1 3.88 us: body(): down_diff = down_anchor - down_local[0]]
  transfers between devices with their start and end apart: 3 -> 3, of which waited for: 2 -> 2; matrix products, arithmetic and copies ran while one was open for 3% -> 0% of each run, Pallas kernels for 0% -> 36%
where the time goes in v3:
time: 76.4 us; the launch traced here: 75.5 us
  Pallas kernels  48.1 us (63%)
  waiting for transfers between devices  17.8 us (23%)
  local copies, waits for them, and re-layouts  5.45 us (7%)
  starting transfers between devices  3.29 us (4%)
  between operations  0.78 us (1%)
    pallas_call x1, Pallas kernels, body(): pl.pallas_call(reduce_factors, out_shape=V(tall + 8, span), in_specs=[any...  20 us
    pallas_call x1, Pallas kernels, body(): pl.pallas_call(gather_factors, out_shape=[V(2 * SIDE, rank, span), V(*nor...  17.1 us
    ppermute x1, waiting for transfers between devices, body(): peer_part = lax.ppermute(part, 'group', swap)  17 us
    pallas_call x1, Pallas kernels, body(): pl.pallas_call(rebuild, out_shape=[S(gate_anchor), S(gate_moment), S(norm...  7.06 us
    unnamed x22, local copies, waits for them, and re-layouts  5.45 us
    pallas_call x1, Pallas kernels, body(): pl.pallas_call(own_half, out_shape=[S(down_anchor), S(down_moment), V(hal...  2.44 us
    ppermute x1, starting transfers between devices, body(): peer = lax.ppermute(own, 'group', swap)  1.72 us
  transfers between devices with their start and end apart: 3, of which 2 were waited for; matrix products, arithmetic and copies ran while one was open for 0% of the time, Pallas kernels for 36%

profile of v3, /device:TPU:1, one launch (start us, length us, event | category | flops | bytes accessed | tf_op | source)
XLA Modules:
  0.0 75.5 jit_solution(7812623144796950964)
XLA Ops:
  0.6 0.0 copy-start
  0.6 0.0 copy-start.1
  0.7 1.7 %copy-done.1 = f32[4096,128]{1,0:T(8,128)S(1)} copy-done((f32[4096,128]{1,0:T(8,128)S(1)}, f32[4096,128]{1,0:T(8,128)}, u32[]{:S(2)}) %copy-start.1) | copy-done | bytes 2097176
  2.4 0.0 copy-start.3
  2.4 1.6 %copy-done.3 = f32[1,4096,128]{2,1,0:T(8,128)S(1)} copy-done((f32[1,4096,128]{2,1,0:T(8,128)S(1)}, f32[1,4096,128]{2,1,0:T(8,128)}, u32[]{:S(2)}) %copy-start.3) | copy-done | bytes 2097176
  4.0 0.8 %copy-done.6 = f32[64,128]{1,0:T(8,128)S(1)} copy-done((f32[64,128]{1,0:T(8,128)S(1)}, f32[64,128]{1,0:T(8,128)}, u32[]{:S(2)}) %copy-start.6) | copy-done | bytes 32792
  4.7 0.7 copy-done.8
  5.4 0.7 copy-done.10
  6.1 20.0 %shard_map.146.own = f32[24,512]{1,0:T(8,128)S(1)} custom-call(f32[4096,128]{1,0:T(8,128)S(1)} %copy-done.1, f32[1,4096,128]{2,1,0:T(8,128)S(1)} %copy-done.3, f32[64,128]{1,0:T(8,128)S(1)} %copy-done.6, f32[1,2,64]{2,1,0:T(2,128)S(1)} %copy-done.8, f32[1,64]{1,0:T(1,128)S(1)} %copy-done.10), custom_call_target="tpu_custom_call" | custom-call | bytes 70000000 | tf_op jit(solution)/shard_map/pallas_call | solution.py:326
  26.1 0.0 copy-start.2
  26.1 1.7 %collective-permute-start.1 = (f32[24,512]{1,0:T(8,128)S(1)}, f32[24,512]{1,0:T(8,128)S(1)}, u32[]{:S(2)}, u32[]{:S(2)}) collective-permute-start(f32[24,512]{1,0:T(8,128)S(1)} %shard_map.146.own), channel_id=1, source_target_pairs={{0,64},{64,0},{1,65},{65,1},{2,66},{66,2},{3,67},{67,3},{4,68},{68... | collective-permute-start | bytes 147464 | tf_op jit(solution)/shard_map/ppermute | solution.py:338
  27.8 0.0 copy-done
  27.8 0.1 shard_map.145.raw
  27.9 0.0 copy-start.9
  27.9 0.0 copy-start.4
  27.9 0.0 copy-start.7
  27.9 0.1 collective-permute-start
  28.1 0.0 copy-done.2
  28.1 0.4 shard_map.147.part
  28.4 0.9 %collective-permute-done.1.peer = f32[24,512]{1,0:T(8,128)S(1)} collective-permute-done((f32[24,512]{1,0:T(8,128)S(1)}, f32[24,512]{1,0:T(8,128)S(1)}, u32[]{:S(2)}, u32[]{:S(2)}) %collective-permute-start.1) | collective-permute-done | bytes 49184 | tf_op jit(solution)/shard_map/ppermute | solution.py:338
  29.3 1.5 %collective-permute-start.2 = (f32[128,2048]{1,0:T(8,128)S(1)}, f32[128,2048]{1,0:T(8,128)S(1)}, u32[]{:S(2)}, u32[]{:S(2)}) collective-permute-start(f32[128,2048]{1,0:T(8,128)S(1)} %shard_map.147.part), channel_id=1, source_target_pairs={{0,64},{64,0},{1,65},{65,1},{2,66},{66,2},{3,67},{67,3},{4,68},{68... | collective-permute-start | bytes 3145736 | tf_op jit(solution)/shard_map/ppermute | solution.py:340
  30.8 0.0 copy-done.9
  30.8 17.1 %shard_map.148 = (f32[8,64,512]{2,1,0:T(8,128)S(1)}, f32[2,64]{1,0:T(2,128)S(1)}, f32[1,64]{1,0:T(1,128)S(1)}) custom-call(f32[24,512]{1,0:T(8,128)S(1)} %shard_map.146.own, f32[24,512]{1,0:T(8,128)S(1)} %collective-permute-done.1.peer, f32[2,64]{1,0:T(2,128)S(1)} %copy-done.9), custom_call_target="tpu_custom_call" | custom-call | bytes 52500000 | tf_op jit(solution)/shard_map/pallas_call | solution.py:341
  47.9 0.0 copy-done.4
  47.9 0.0 copy-done.7
  47.9 0.0 copy-start.5
  47.9 7.1 %shard_map.151 = (f32[4096,128]{1,0:T(8,128)}, f32[4096,128]{1,0:T(8,128)}, f32[2,64]{1,0:T(2,128)}, f32[1,64]{1,0:T(1,128)}) custom-call(f32[4096,128]{1,0:T(8,128)S(1)} %copy-done.1, f32[4096,128]{1,0:T(8,128)S(1)} %copy-done.4, f32[64,128]{1,0:T(8,128)S(1)} %copy-done.7, f32[8,64,512]{2,1,0:T(8,128)S(1)} %get-tuple-element.20.whole, ...), custom_call_target="tpu_custom_call" | custom-call | bytes 17500000 | tf_op jit(solution)/shard_map/pallas_call | solution.py:349
  55.0 0.0 collective-permute-done.peer
  55.0 0.0 copy-done.5
  55.0 2.4 %shard_map.149 = (f32[256,2048]{1,0:T(8,128)}, f32[128,2048]{1,0:T(8,128)}, f32[128,2048]{1,0:T(8,128)S(1)}) custom-call(f32[256,2048]{1,0:T(8,128)S(1)} %copy-done.5, f32[128,2048]{1,0:T(8,128)S(1)} %copy-done.2, f32[128,2048]{1,0:T(8,128)S(1)} %shard_map.145.raw, f32[128,2048]{1,0:T(8,128)S(1)} %collective-permute-done.peer, f32[1,256,2048]{2,1,0:T(8,128)S(1)} %copy-done, ...), custom_call_target="tpu_custom_call" | custom-call | bytes 14000000 | tf_op jit(solution)/shard_map/pallas_call | solution.py:358
  57.5 17.0 %collective-permute-done.2.peer = f32[128,2048]{1,0:T(8,128)S(1)} collective-permute-done((f32[128,2048]{1,0:T(8,128)S(1)}, f32[128,2048]{1,0:T(8,128)S(1)}, u32[]{:S(2)}, u32[]{:S(2)}) %collective-permute-start.2) | collective-permute-done | bytes 1048608 | tf_op jit(solution)/shard_map/ppermute | solution.py:340
  74.4 1.0 %shard_map.150 = f32[256,2048]{1,0:T(8,128)} custom-call(f32[256,2048]{1,0:T(8,128)} %get-tuple-element.23.given, f32[128,2048]{1,0:T(8,128)S(1)} %get-tuple-element.24.base, f32[128,2048]{1,0:T(8,128)S(1)} %collective-permute-done.2.peer), custom_call_target="tpu_custom_call", output_to_operand_aliasing={{}: (0, {})} | custom-call | bytes 3500000 | tf_op jit(solution)/shard_map/pallas_call | solution.py:366
  (3 shorter events, 0.0 us)
Async XLA Ops:
  0.6 27.2 %copy-start = (f32[1,256,2048]{2,1,0:T(8,128)S(1)}, f32[1,256,2048]{2,1,0:T(8,128)}, u32[]{:S(2)}) copy-start(f32[1,256,2048]{2,1,0:T(8,128)} %down_local.5) | copy-start | bytes 6291460
  0.6 1.7 %copy-start.1 = (f32[4096,128]{1,0:T(8,128)S(1)}, f32[4096,128]{1,0:T(8,128)}, u32[]{:S(2)}) copy-start(f32[4096,128]{1,0:T(8,128)} %gate_anchor.3) | copy-start | bytes 6291460
  2.4 1.6 %copy-start.3 = (f32[1,4096,128]{2,1,0:T(8,128)S(1)}, f32[1,4096,128]{2,1,0:T(8,128)}, u32[]{:S(2)}) copy-start(f32[1,4096,128]{2,1,0:T(8,128)} %gate_local.1) | copy-start | bytes 6291460
  4.0 0.8 %copy-start.6 = (f32[64,128]{1,0:T(8,128)S(1)}, f32[64,128]{1,0:T(8,128)}, u32[]{:S(2)}) copy-start(f32[64,128]{1,0:T(8,128)} %factor_basis.3) | copy-start | bytes 98308
  4.7 0.7 copy-start.8
  5.4 0.7 copy-start.10
  26.1 2.0 %copy-start.2 = (f32[128,2048]{1,0:T(8,128)S(1)}, f32[128,2048]{1,0:T(8,128)}, u32[]{:S(2)}) copy-start(f32[128,2048]{1,0:T(8,128)} %down_moment.3) | copy-start | bytes 3145732
  26.1 3.2 %collective-permute-start.1 = (f32[24,512]{1,0:T(8,128)S(1)}, f32[24,512]{1,0:T(8,128)S(1)}, u32[]{:S(2)}, u32[]{:S(2)}) collective-permute-start(f32[24,512]{1,0:T(8,128)S(1)} %shard_map.146.own), channel_id=1, source_target_pairs={{0,64},{64,0},{1,65},{65,1},{2,66},{66,2},{3,67},{67,3},{4,68},{68... | collective-permute-start | bytes 147464 | tf_op jit(solution)/shard_map/ppermute | solution.py:338
  27.9 2.9 %copy-start.9 = (f32[2,64]{1,0:T(2,128)S(1)}, f32[2,64]{1,0:T(2,128)}, u32[]{:S(2)}) copy-start(f32[2,64]{1,0:T(2,128)} %norm_anchor.1) | copy-start | bytes 1540
  27.9 20.0 %copy-start.4 = (f32[4096,128]{1,0:T(8,128)S(1)}, f32[4096,128]{1,0:T(8,128)}, u32[]{:S(2)}) copy-start(f32[4096,128]{1,0:T(8,128)} %gate_moment.1) | copy-start | bytes 6291460
  27.9 20.0 %copy-start.7 = (f32[64,128]{1,0:T(8,128)S(1)}, f32[64,128]{1,0:T(8,128)}, u32[]{:S(2)}) copy-start(f32[64,128]{1,0:T(8,128)} %factor_basis.3) | copy-start | bytes 98308
  27.9 27.1 %collective-permute-start = (f32[128,2048]{1,0:T(8,128)S(1)}, f32[128,2048]{1,0:T(8,128)S(1)}, u32[]{:S(2)}, u32[]{:S(2)}) collective-permute-start(f32[128,2048]{1,0:T(8,128)S(1)} %shard_map.145.raw), channel_id=1, source_target_pairs={{0,64},{64,0},{1,65},{65,1},{2,66},{66,2},{3,67},{67,3},{4,68},{68... | collective-permute-start | bytes 3145736 | tf_op jit(solution)/shard_map/ppermute | solution.py:321
  29.3 45.2 %collective-permute-start.2 = (f32[128,2048]{1,0:T(8,128)S(1)}, f32[128,2048]{1,0:T(8,128)S(1)}, u32[]{:S(2)}, u32[]{:S(2)}) collective-permute-start(f32[128,2048]{1,0:T(8,128)S(1)} %shard_map.147.part), channel_id=1, source_target_pairs={{0,64},{64,0},{1,65},{65,1},{2,66},{66,2},{3,67},{67,3},{4,68},{68... | collective-permute-start | bytes 3145736 | tf_op jit(solution)/shard_map/ppermute | solution.py:340
  47.9 7.1 %copy-start.5 = (f32[256,2048]{1,0:T(8,128)S(1)}, f32[256,2048]{1,0:T(8,128)}, u32[]{:S(2)}) copy-start(f32[256,2048]{1,0:T(8,128)} %down_anchor.1) | copy-start | bytes 6291460

commit v4 on v3

--- a/solution.py
+++ b/solution.py
@@ -75,7 +75,7 @@
 
 def reduce_factors(
     gate_anchor, gate_local, factor_basis, norm_local, norm_moment, out,
-    ga, gl, basis, away, home, from_core, from_x, row, from_y,
+    ga, gl, basis, away, home, from_core, from_x, via, row, from_y,
     load_sem, core_send, core_recv, x_send, x_recv, y_send, y_recv,
 ):
     s = lax.axis_index("shard")
@@ -97,7 +97,7 @@
     loads = [pltpu.make_async_copy(src, dst, load_sem.at[i]) for i, (src, dst) in enumerate(pairs)]
     for load in loads:
         load.start()
-    meet([other_core] + [along_x(d) for d in range(1, SIDE)] + [along_y(d) for d in range(1, SIDE)])
+    meet([other_core, along_x(1), along_x(3)] + [along_y(d) for d in range(1, SIDE)])
 
     def factor(start, target):
         def block(i, carry):
@@ -122,16 +122,34 @@
     out[tall : tall + 2, 0 : norm_local.shape[2]] = norm_local[0]
     out[tall + 2 : tall + 3, 0 : norm_local.shape[2]] = norm_moment[...]
     core_copy.wait_recv()
-    x_copies = []
-    for d in (2, 1, 3):
-        to = (x + d) % SIDE
-        home[to] = home[to] + from_core[to]
-        x_copies.append(remote(home.at[to], from_x.at[d - 1], x_send.at[d - 1], x_recv.at[d - 1], along_x(d)))
-        x_copies[-1].start()
+    rank = row.shape[0]
+    top, low = pl.ds(0, rank // 2), pl.ds(rank // 2, rank // 2)
+    up, across, down = (x + 1) % SIDE, (x + 2) % SIDE, (x + 3) % SIDE
+
+    def send_x(i, src, dst, d):
+        copy = remote(src, dst, x_send.at[i], x_recv.at[i], along_x(d))
+        copy.start()
+        return copy
+
+    home[across] = home[across] + from_core[across]
+    x_copies = [
+        send_x(0, home.at[across, top], via.at[0], 1),
+        send_x(1, home.at[across, low], via.at[1], 3),
+    ]
+    home[up] = home[up] + from_core[up]
+    x_copies.append(send_x(2, home.at[up, low], from_x.at[0, low], 1))
+    home[down] = home[down] + from_core[down]
+    x_copies.append(send_x(3, home.at[down, top], from_x.at[1, top], 3))
     row[...] = home[x] + from_core[x]
-    for copy in x_copies:
+    x_copies[0].wait_recv()
+    home[up, top, :] = home[up, top, :] + via[0]
+    x_copies.append(send_x(4, home.at[up, top], from_x.at[0, top], 1))
+    x_copies[1].wait_recv()
+    home[down, low, :] = home[down, low, :] + via[1]
+    x_copies.append(send_x(5, home.at[down, low], from_x.at[1, low], 3))
+    for copy in x_copies[2:]:
         copy.wait_recv()
-    row[...] = (row[...] + from_x[0]) + (from_x[1] + from_x[2])
+    row[...] = row[...] + (from_x[0] + from_x[1])
     y_copies = []
     for d in (2, 1, 3):
         rows = pl.ds(pl.multiple_of(((y + d) % SIDE) * tall, tall), tall)
@@ -197,19 +215,15 @@
 
 def rebuild(
     gate_anchor, gate_moment, factor_basis, whole, norm_a, norm_m,
-    new_anchor, new_moment, new_norm_anchor, new_norm_moment, ga, gm, load_sem, store_sem,
+    new_anchor, new_moment, new_norm_anchor, new_norm_moment, ga, gm, store_sem,
 ):
     blocks = whole.shape[0]
     span = whole.shape[2]
-    loads, stores = [], []
+    stores = []
     for i in range(blocks):
         rows = pl.ds(i * span, span)
-        loads.append(pltpu.make_async_copy(gate_anchor.at[rows], ga.at[rows], load_sem.at[2 * i]))
-        loads.append(pltpu.make_async_copy(gate_moment.at[rows], gm.at[rows], load_sem.at[2 * i + 1]))
         stores.append(pltpu.make_async_copy(ga.at[rows], new_anchor.at[rows], store_sem.at[2 * i]))
         stores.append(pltpu.make_async_copy(gm.at[rows], new_moment.at[rows], store_sem.at[2 * i + 1]))
-    for load in loads:
-        load.start()
     new_norm_anchor[...] = norm_a[...]
     new_norm_moment[...] = norm_m[...]
     for i in range(blocks):
@@ -218,11 +232,9 @@
             whole[i], factor_basis[...], (((0,), (0,)), ((), ())), precision=HIGHEST,
             preferred_element_type=jnp.float32,
         )
-        loads[2 * i].wait()
-        loads[2 * i + 1].wait()
-        moment = momentum * gm[rows, :] + delta
+        moment = momentum * gate_moment[rows, :] + delta
         gm[rows, :] = moment
-        ga[rows, :] = ga[rows, :] - outer_rate * (delta + momentum * moment)
+        ga[rows, :] = gate_anchor[rows, :] - outer_rate * (delta + momentum * moment)
         stores[2 * i].start()
         stores[2 * i + 1].start()
     for store in stores:
@@ -316,7 +328,7 @@
 
     raw = pl.pallas_call(
         take_raw, out_shape=V(half, width), in_specs=[pl.BlockSpec(memory_space=pltpu.HBM)], out_specs=vmem, scratch_shapes=[dma],
-        compiler_params=params(8), cost_estimate=cost(1),
+        compiler_params=params(60), cost_estimate=cost(1),
     )(down_local)
     peer_raw = lax.ppermute(raw, "group", swap)
     part = pl.pallas_call(
@@ -330,13 +342,22 @@
         out_specs=vmem,
         scratch_shapes=[
             V(hidden, depth), V(hidden, depth), V(rank, depth), V(SIDE, rank, span), V(SIDE, rank, span),
-            V(SIDE, rank, span), V(SIDE - 1, rank, span), V(rank, span), V(SIDE - 1, tall, span),
-            dma((5,)), dma, dma, dma((3,)), dma((3,)), dma((3,)), dma((3,)),
+            V(SIDE, rank, span), V(2, rank, span), V(2, rank // 2, span), V(rank, span), V(SIDE - 1, tall, span),
+            dma((5,)), dma, dma, dma((6,)), dma((6,)), dma((3,)), dma((3,)),
         ],
         compiler_params=params(16, collective_id=0, has_side_effects=True), cost_estimate=cost(20),
     )(gate_anchor, gate_local, factor_basis, norm_local, norm_moment)
     peer = lax.ppermute(own, "group", swap)
-    peer, part = lax.optimization_barrier((peer, part))
+    peer_raw, _ = lax.optimization_barrier((peer_raw, own))
+    anchor, new_down_moment, base = pl.pallas_call(
+        own_half,
+        out_shape=[S(down_anchor), S(down_moment), V(half, width)],
+        in_specs=[anywhere] * 2 + [vmem, anywhere, anywhere, vmem],
+        out_specs=[anywhere] * 2 + [vmem],
+        scratch_shapes=[V(2 * half, width)] + [V(half, width)] * 3 + [dma((4,)), dma((2,))],
+        compiler_params=params(16), cost_estimate=cost(4),
+    )(down_anchor, down_moment, raw, peer_raw, down_local, part)
+    peer, base, part = lax.optimization_barrier((peer, base, part))
     peer_part = lax.ppermute(part, "group", swap)
     whole, norm_a, norm_m = pl.pallas_call(
         gather_factors,
@@ -349,20 +370,11 @@
     new_gate_anchor, new_gate_moment, new_norm_anchor, new_norm_moment = pl.pallas_call(
         rebuild,
         out_shape=[S(gate_anchor), S(gate_moment), S(norm_anchor), S(norm_moment)],
-        in_specs=[anywhere] * 2 + [vmem] * 4,
+        in_specs=[vmem] * 6,
         out_specs=[anywhere] * 2 + [vmem] * 2,
-        scratch_shapes=[V(hidden, depth), V(hidden, depth), dma((4 * SIDE,)), dma((4 * SIDE,))],
+        scratch_shapes=[V(hidden, depth), V(hidden, depth), dma((4 * SIDE,))],
         compiler_params=params(16), cost_estimate=cost(5),
     )(gate_anchor, gate_moment, factor_basis, whole, norm_a, norm_m)
-    peer_raw, _ = lax.optimization_barrier((peer_raw, whole))
-    anchor, new_down_moment, base = pl.pallas_call(
-        own_half,
-        out_shape=[S(down_anchor), S(down_moment), V(half, width)],
-        in_specs=[anywhere] * 2 + [vmem, anywhere, anywhere, vmem],
-        out_specs=[anywhere] * 2 + [vmem],
-        scratch_shapes=[V(2 * half, width)] + [V(half, width)] * 3 + [dma((4,)), dma((2,))],
-        compiler_params=params(16), cost_estimate=cost(4),
-    )(down_anchor, down_moment, raw, peer_raw, down_local, part)
     new_down_anchor = pl.pallas_call(
         other_half,
         out_shape=S(down_anchor),

time: 76.4 us -> 55.4 us (0.73)
  waiting for transfers between devices: 17.8 us -> 2.94 us
  local copies, waits for them, and re-layouts: 5.45 us -> 1.63 us
  Pallas kernels: 48.1 us -> 44.8 us
  starting transfers between devices: 3.29 us -> 4.2 us
    ppermute x1, waiting for transfers between devices: 17 us -> 0.01 us  [body(): peer_part = lax.ppermute(part, 'group', swap)]
    unnamed x22 -> x20, local copies, waits for them, and re-layouts: 5.45 us -> 1.63 us
    pallas_call x1, Pallas kernels: 7.06 us -> 3.96 us  [body(): pl.pallas_call(rebuild, out_shape=[S(gate_anchor), S(gate_moment), S(norm...]
    ppermute x1, waiting for transfers between devices: 0.01 us -> 2.93 us  [body(): peer_raw = lax.ppermute(raw, 'group', swap)]
    pallas_call x1, Pallas kernels: 20 us -> 17.5 us  [body(): pl.pallas_call(reduce_factors, out_shape=V(tall + 8, span), in_specs=[any...]
    ppermute x1, starting transfers between devices: 0.11 us -> 2.55 us  [body(): peer_raw = lax.ppermute(raw, 'group', swap)]
    pallas_call x1, Pallas kernels: 0.08 us -> 1.39 us  [body(): pl.pallas_call(take_raw, out_shape=V(half, width), in_specs=[pl.BlockSpec...]
    ppermute x1, starting transfers between devices: 1.72 us -> 0.41 us  [body(): peer = lax.ppermute(own, 'group', swap)]
  transfers between devices with their start and end apart: 3 -> 3, of which waited for: 2 -> 1; matrix products, arithmetic and copies ran while one was open for 0% -> 0% of each run, Pallas kernels for 36% -> 78%
where the time goes in v4:
time: 55.4 us; the launch traced here: 54.4 us
  Pallas kernels  44.8 us (81%)
  starting transfers between devices  4.2 us (8%)
  waiting for transfers between devices  2.94 us (5%)
  local copies, waits for them, and re-layouts  1.63 us (3%)
  between operations  0.79 us (1%)
    pallas_call x1, Pallas kernels, body(): pl.pallas_call(gather_factors, out_shape=[V(2 * SIDE, rank, span), V(*nor...  18.1 us
    pallas_call x1, Pallas kernels, body(): pl.pallas_call(reduce_factors, out_shape=V(tall + 8, span), in_specs=[any...  17.5 us
    pallas_call x1, Pallas kernels, body(): pl.pallas_call(rebuild, out_shape=[S(gate_anchor), S(gate_moment), S(norm...  3.96 us
    ppermute x1, waiting for transfers between devices, body(): peer_raw = lax.ppermute(raw, 'group', swap)  2.93 us
    ppermute x1, starting transfers between devices, body(): peer_raw = lax.ppermute(raw, 'group', swap)  2.55 us
    pallas_call x1, Pallas kernels, body(): pl.pallas_call(own_half, out_shape=[S(down_anchor), S(down_moment), V(hal...  2.43 us
    unnamed x20, local copies, waits for them, and re-layouts  1.63 us
    pallas_call x1, Pallas kernels, body(): pl.pallas_call(take_raw, out_shape=V(half, width), in_specs=[pl.BlockSpec...  1.39 us
  transfers between devices with their start and end apart: 3, of which 1 were waited for; matrix products, arithmetic and copies ran while one was open for 0% of the time, Pallas kernels for 78%

profile of v4, /device:TPU:1, one launch (start us, length us, event | category | flops | bytes accessed | tf_op | source)
XLA Modules:
  0.0 54.4 jit_solution(17909943375475482937)
XLA Ops:
  0.6 0.0 copy-start.6
  0.6 0.0 copy-start.1
  0.7 0.0 copy-start.9
  0.7 0.0 copy-start.7
  0.7 1.4 %shard_map.145.raw = f32[128,2048]{1,0:T(8,128)S(1)} custom-call(f32[1,256,2048]{2,1,0:T(8,128)} %down_local.5), custom_call_target="tpu_custom_call" | custom-call | bytes 3500000 | tf_op jit(solution)/shard_map/pallas_call | solution.py:329
  2.1 0.0 copy-start
  2.1 0.0 copy-start.2
  2.1 2.5 %collective-permute-start = (f32[128,2048]{1,0:T(8,128)S(1)}, f32[128,2048]{1,0:T(8,128)S(1)}, u32[]{:S(2)}, u32[]{:S(2)}) collective-permute-start(f32[128,2048]{1,0:T(8,128)S(1)} %shard_map.145.raw), channel_id=1, source_target_pairs={{0,64},{64,0},{1,65},{65,1},{2,66},{66,2},{3,67},{67,3},{4,68},{68... | collective-permute-start | bytes 3145736 | tf_op jit(solution)/shard_map/ppermute | solution.py:333
  4.6 0.0 copy-done.6
  4.6 0.0 copy-done.1
  4.6 0.0 copy-done.9
  4.6 0.0 copy-done.7
  4.7 0.0 copy-start.3
  4.7 1.6 %copy-done.3 = f32[1,4096,128]{2,1,0:T(8,128)S(1)} copy-done((f32[1,4096,128]{2,1,0:T(8,128)S(1)}, f32[1,4096,128]{2,1,0:T(8,128)}, u32[]{:S(2)}) %copy-start.3) | copy-done | bytes 2097176
  6.2 17.5 %shard_map.146.own = f32[24,512]{1,0:T(8,128)S(1)} custom-call(f32[4096,128]{1,0:T(8,128)S(1)} %copy-done.1, f32[1,4096,128]{2,1,0:T(8,128)S(1)} %copy-done.3, f32[64,128]{1,0:T(8,128)S(1)} %copy-done.6, f32[1,2,64]{2,1,0:T(2,128)S(1)} %copy-done.7, f32[1,64]{1,0:T(1,128)S(1)} %copy-done.9), custom_call_target="tpu_custom_call" | custom-call | bytes 70000000 | tf_op jit(solution)/shard_map/pallas_call | solution.py:338
  23.8 0.0 copy-start.5
  23.8 0.4 collective-permute-start.1
  24.2 0.0 copy-done
  24.2 0.0 copy-done.2
  24.2 0.4 shard_map.147.part
  24.5 0.0 copy-start.8
  24.6 0.0 copy-start.4
  24.6 2.9 %collective-permute-done.peer = f32[128,2048]{1,0:T(8,128)S(1)} collective-permute-done((f32[128,2048]{1,0:T(8,128)S(1)}, f32[128,2048]{1,0:T(8,128)S(1)}, u32[]{:S(2)}, u32[]{:S(2)}) %collective-permute-start) | collective-permute-done | bytes 1048608 | tf_op jit(solution)/shard_map/ppermute | solution.py:333
  27.5 0.0 copy-done.5
  27.5 2.4 %shard_map.148 = (f32[256,2048]{1,0:T(8,128)}, f32[128,2048]{1,0:T(8,128)}, f32[128,2048]{1,0:T(8,128)S(1)}) custom-call(f32[256,2048]{1,0:T(8,128)S(1)} %copy-done.5, f32[128,2048]{1,0:T(8,128)S(1)} %copy-done.2, f32[128,2048]{1,0:T(8,128)S(1)} %shard_map.145.raw, f32[128,2048]{1,0:T(8,128)S(1)} %collective-permute-done.peer, f32[1,256,2048]{2,1,0:T(8,128)S(1)} %copy-done, ...), custom_call_target="tpu_custom_call" | custom-call | bytes 14000000 | tf_op jit(solution)/shard_map/pallas_call | solution.py:352
  29.9 0.0 collective-permute-done.1.peer
  30.0 1.2 %collective-permute-start.2 = (f32[128,2048]{1,0:T(8,128)S(1)}, f32[128,2048]{1,0:T(8,128)S(1)}, u32[]{:S(2)}, u32[]{:S(2)}) collective-permute-start(f32[128,2048]{1,0:T(8,128)S(1)} %shard_map.147.part), channel_id=1, source_target_pairs={{0,64},{64,0},{1,65},{65,1},{2,66},{66,2},{3,67},{67,3},{4,68},{68... | collective-permute-start | bytes 3145736 | tf_op jit(solution)/shard_map/ppermute | solution.py:361
  31.2 0.0 copy-done.8
  31.2 18.1 %shard_map.150 = (f32[8,64,512]{2,1,0:T(8,128)S(1)}, f32[2,64]{1,0:T(2,128)S(1)}, f32[1,64]{1,0:T(1,128)S(1)}) custom-call(f32[24,512]{1,0:T(8,128)S(1)} %shard_map.146.own, f32[24,512]{1,0:T(8,128)S(1)} %collective-permute-done.1.peer, f32[2,64]{1,0:T(2,128)S(1)} %copy-done.8), custom_call_target="tpu_custom_call" | custom-call | bytes 52500000 | tf_op jit(solution)/shard_map/pallas_call | solution.py:362
  49.3 4.0 %shard_map.151 = (f32[4096,128]{1,0:T(8,128)}, f32[4096,128]{1,0:T(8,128)}, f32[2,64]{1,0:T(2,128)}, f32[1,64]{1,0:T(1,128)}) custom-call(f32[4096,128]{1,0:T(8,128)S(1)} %copy-done.1, f32[4096,128]{1,0:T(8,128)S(1)} %copy-done.4, f32[64,128]{1,0:T(8,128)S(1)} %copy-done.6, f32[8,64,512]{2,1,0:T(8,128)S(1)} %get-tuple-element.27.whole, ...), custom_call_target="tpu_custom_call" | custom-call | bytes 17500000 | tf_op jit(solution)/shard_map/pallas_call | solution.py:370
  53.3 0.0 collective-permute-done.2.peer
  53.3 1.1 %shard_map.149 = f32[256,2048]{1,0:T(8,128)} custom-call(f32[256,2048]{1,0:T(8,128)} %get-tuple-element.21.given, f32[128,2048]{1,0:T(8,128)S(1)} %get-tuple-element.23.base, f32[128,2048]{1,0:T(8,128)S(1)} %collective-permute-done.2.peer), custom_call_target="tpu_custom_call", output_to_operand_aliasing={{}: (0, {})} | custom-call | bytes 3500000 | tf_op jit(solution)/shard_map/pallas_call | solution.py:378
  (1 shorter events, 0.0 us)
Async XLA Ops:
  0.6 4.0 %copy-start.6 = (f32[64,128]{1,0:T(8,128)S(1)}, f32[64,128]{1,0:T(8,128)}, u32[]{:S(2)}) copy-start(f32[64,128]{1,0:T(8,128)} %factor_basis.3) | copy-start | bytes 98308
  0.6 4.0 %copy-start.1 = (f32[4096,128]{1,0:T(8,128)S(1)}, f32[4096,128]{1,0:T(8,128)}, u32[]{:S(2)}) copy-start(f32[4096,128]{1,0:T(8,128)} %gate_anchor.3) | copy-start | bytes 6291460
  0.7 4.0 %copy-start.9 = (f32[1,64]{1,0:T(1,128)S(1)}, f32[1,64]{1,0:T(1,128)}, u32[]{:S(2)}) copy-start(f32[1,64]{1,0:T(1,128)} %norm_moment.1) | copy-start | bytes 772
  0.7 4.0 %copy-start.7 = (f32[1,2,64]{2,1,0:T(2,128)S(1)}, f32[1,2,64]{2,1,0:T(2,128)}, u32[]{:S(2)}) copy-start(f32[1,2,64]{2,1,0:T(2,128)} %norm_local.1) | copy-start | bytes 1540
  2.1 22.1 %copy-start = (f32[1,256,2048]{2,1,0:T(8,128)S(1)}, f32[1,256,2048]{2,1,0:T(8,128)}, u32[]{:S(2)}) copy-start(f32[1,256,2048]{2,1,0:T(8,128)} %down_local.5) | copy-start | bytes 6291460
  2.1 22.1 %copy-start.2 = (f32[128,2048]{1,0:T(8,128)S(1)}, f32[128,2048]{1,0:T(8,128)}, u32[]{:S(2)}) copy-start(f32[128,2048]{1,0:T(8,128)} %down_moment.3) | copy-start | bytes 3145732
  2.1 25.4 %collective-permute-start = (f32[128,2048]{1,0:T(8,128)S(1)}, f32[128,2048]{1,0:T(8,128)S(1)}, u32[]{:S(2)}, u32[]{:S(2)}) collective-permute-start(f32[128,2048]{1,0:T(8,128)S(1)} %shard_map.145.raw), channel_id=1, source_target_pairs={{0,64},{64,0},{1,65},{65,1},{2,66},{66,2},{3,67},{67,3},{4,68},{68... | collective-permute-start | bytes 3145736 | tf_op jit(solution)/shard_map/ppermute | solution.py:333
  4.7 1.6 %copy-start.3 = (f32[1,4096,128]{2,1,0:T(8,128)S(1)}, f32[1,4096,128]{2,1,0:T(8,128)}, u32[]{:S(2)}) copy-start(f32[1,4096,128]{2,1,0:T(8,128)} %gate_local.1) | copy-start | bytes 6291460
  23.8 3.8 %copy-start.5 = (f32[256,2048]{1,0:T(8,128)S(1)}, f32[256,2048]{1,0:T(8,128)}, u32[]{:S(2)}) copy-start(f32[256,2048]{1,0:T(8,128)} %down_anchor.1) | copy-start | bytes 6291460
  23.8 6.2 %collective-permute-start.1 = (f32[24,512]{1,0:T(8,128)S(1)}, f32[24,512]{1,0:T(8,128)S(1)}, u32[]{:S(2)}, u32[]{:S(2)}) collective-permute-start(f32[24,512]{1,0:T(8,128)S(1)} %shard_map.146.own), channel_id=1, source_target_pairs={{0,64},{64,0},{1,65},{65,1},{2,66},{66,2},{3,67},{67,3},{4,68},{68... | collective-permute-start | bytes 147464 | tf_op jit(solution)/shard_map/ppermute | solution.py:350
  24.5 6.7 %copy-start.8 = (f32[2,64]{1,0:T(2,128)S(1)}, f32[2,64]{1,0:T(2,128)}, u32[]{:S(2)}) copy-start(f32[2,64]{1,0:T(2,128)} %norm_anchor.1) | copy-start | bytes 1540
  24.6 24.8 %copy-start.4 = (f32[4096,128]{1,0:T(8,128)S(1)}, f32[4096,128]{1,0:T(8,128)}, u32[]{:S(2)}) copy-start(f32[4096,128]{1,0:T(8,128)} %gate_moment.1) | copy-start | bytes 6291460
  30.0 23.3 %collective-permute-start.2 = (f32[128,2048]{1,0:T(8,128)S(1)}, f32[128,2048]{1,0:T(8,128)S(1)}, u32[]{:S(2)}, u32[]{:S(2)}) collective-permute-start(f32[128,2048]{1,0:T(8,128)S(1)} %shard_map.147.part), channel_id=1, source_target_pairs={{0,64},{64,0},{1,65},{65,1},{2,66},{66,2},{3,67},{67,3},{4,68},{68... | collective-permute-start | bytes 3145736 | tf_op jit(solution)/shard_map/ppermute | solution.py:361

commit v5 on v4

--- a/solution.py
+++ b/solution.py
@@ -348,16 +348,7 @@
         compiler_params=params(16, collective_id=0, has_side_effects=True), cost_estimate=cost(20),
     )(gate_anchor, gate_local, factor_basis, norm_local, norm_moment)
     peer = lax.ppermute(own, "group", swap)
-    peer_raw, _ = lax.optimization_barrier((peer_raw, own))
-    anchor, new_down_moment, base = pl.pallas_call(
-        own_half,
-        out_shape=[S(down_anchor), S(down_moment), V(half, width)],
-        in_specs=[anywhere] * 2 + [vmem, anywhere, anywhere, vmem],
-        out_specs=[anywhere] * 2 + [vmem],
-        scratch_shapes=[V(2 * half, width)] + [V(half, width)] * 3 + [dma((4,)), dma((2,))],
-        compiler_params=params(16), cost_estimate=cost(4),
-    )(down_anchor, down_moment, raw, peer_raw, down_local, part)
-    peer, base, part = lax.optimization_barrier((peer, base, part))
+    peer, peer_raw, part = lax.optimization_barrier((peer, peer_raw, part))
     peer_part = lax.ppermute(part, "group", swap)
     whole, norm_a, norm_m = pl.pallas_call(
         gather_factors,
@@ -375,6 +366,15 @@
         scratch_shapes=[V(hidden, depth), V(hidden, depth), dma((4 * SIDE,))],
         compiler_params=params(16), cost_estimate=cost(5),
     )(gate_anchor, gate_moment, factor_basis, whole, norm_a, norm_m)
+    peer_raw, _ = lax.optimization_barrier((peer_raw, whole))
+    anchor, new_down_moment, base = pl.pallas_call(
+        own_half,
+        out_shape=[S(down_anchor), S(down_moment), V(half, width)],
+        in_specs=[anywhere] * 2 + [vmem, anywhere, anywhere, vmem],
+        out_specs=[anywhere] * 2 + [vmem],
+        scratch_shapes=[V(2 * half, width)] + [V(half, width)] * 3 + [dma((4,)), dma((2,))],
+        compiler_params=params(16), cost_estimate=cost(4),
+    )(down_anchor, down_moment, raw, peer_raw, down_local, part)
     new_down_anchor = pl.pallas_call(
         other_half,
         out_shape=S(down_anchor),

time: 55.4 us -> 55 us (level); the launches traced: 54.4 us -> 54.8 us
  waiting for transfers between devices: 2.94 us -> 4.02 us
    ppermute x1, waiting for transfers between devices: 0.01 us -> 4.02 us  [body(): peer = lax.ppermute(own, 'group', swap)]
    ppermute x1, waiting for transfers between devices: 2.93 us -> 0.01 us  [body(): peer_raw = lax.ppermute(raw, 'group', swap)]
  transfers between devices with their start and end apart: 3 -> 3, of which waited for: 1 -> 1; matrix products, arithmetic and copies ran while one was open for 0% -> 0% of each run, Pallas kernels for 78% -> 76%
where the time goes in v5:
time: 55 us; the launch traced here: 54.8 us
  Pallas kernels  44.3 us (81%)
  starting transfers between devices  4.11 us (7%)
  waiting for transfers between devices  4.02 us (7%)
  local copies, waits for them, and re-layouts  1.63 us (3%)
  between operations  0.79 us (1%)
    pallas_call x1, Pallas kernels, body(): pl.pallas_call(gather_factors, out_shape=[V(2 * SIDE, rank, span), V(*nor...  17.6 us
    pallas_call x1, Pallas kernels, body(): pl.pallas_call(reduce_factors, out_shape=V(tall + 8, span), in_specs=[any...  17.5 us
    ppermute x1, waiting for transfers between devices, body(): peer = lax.ppermute(own, 'group', swap)  4.02 us
    pallas_call x1, Pallas kernels, body(): pl.pallas_call(rebuild, out_shape=[S(gate_anchor), S(gate_moment), S(norm...  3.96 us
    ppermute x1, starting transfers between devices, body(): peer_raw = lax.ppermute(raw, 'group', swap)  2.55 us
    pallas_call x1, Pallas kernels, body(): pl.pallas_call(own_half, out_shape=[S(down_anchor), S(down_moment), V(hal...  2.44 us
    unnamed x20, local copies, waits for them, and re-layouts  1.63 us
    pallas_call x1, Pallas kernels, body(): pl.pallas_call(take_raw, out_shape=V(half, width), in_specs=[pl.BlockSpec...  1.39 us
  transfers between devices with their start and end apart: 3, of which 1 were waited for; matrix products, arithmetic and copies ran while one was open for 0% of the time, Pallas kernels for 76%

profile of v5, /device:TPU:1, one launch (start us, length us, event | category | flops | bytes accessed | tf_op | source)
XLA Modules:
  0.0 54.8 jit_solution(13665434292583785534)
XLA Ops:
  0.6 0.0 copy-start.1
  0.6 0.0 copy-start.6
  0.7 0.0 copy-start.7
  0.7 0.0 copy-start.9
  0.7 1.4 %shard_map.145.raw = f32[128,2048]{1,0:T(8,128)S(1)} custom-call(f32[1,256,2048]{2,1,0:T(8,128)} %down_local.5), custom_call_target="tpu_custom_call" | custom-call | bytes 3500000 | tf_op jit(solution)/shard_map/pallas_call | solution.py:329
  2.1 0.0 copy-start
  2.1 0.0 copy-start.2
  2.1 2.5 %collective-permute-start.1 = (f32[128,2048]{1,0:T(8,128)S(1)}, f32[128,2048]{1,0:T(8,128)S(1)}, u32[]{:S(2)}, u32[]{:S(2)}) collective-permute-start(f32[128,2048]{1,0:T(8,128)S(1)} %shard_map.145.raw), channel_id=1, source_target_pairs={{0,64},{64,0},{1,65},{65,1},{2,66},{66,2},{3,67},{67,3},{4,68},{68... | collective-permute-start | bytes 3145736 | tf_op jit(solution)/shard_map/ppermute | solution.py:333
  4.6 0.0 copy-done.1
  4.6 0.0 copy-done.6
  4.6 0.0 copy-done.7
  4.6 0.0 copy-done.9
  4.7 0.0 copy-start.3
  4.7 1.6 %copy-done.3 = f32[1,4096,128]{2,1,0:T(8,128)S(1)} copy-done((f32[1,4096,128]{2,1,0:T(8,128)S(1)}, f32[1,4096,128]{2,1,0:T(8,128)}, u32[]{:S(2)}) %copy-start.3) | copy-done | bytes 2097176
  6.2 17.5 %shard_map.146.own = f32[24,512]{1,0:T(8,128)S(1)} custom-call(f32[4096,128]{1,0:T(8,128)S(1)} %copy-done.1, f32[1,4096,128]{2,1,0:T(8,128)S(1)} %copy-done.3, f32[64,128]{1,0:T(8,128)S(1)} %copy-done.6, f32[1,2,64]{2,1,0:T(2,128)S(1)} %copy-done.7, f32[1,64]{1,0:T(1,128)S(1)} %copy-done.9), custom_call_target="tpu_custom_call" | custom-call | bytes 70000000 | tf_op jit(solution)/shard_map/pallas_call | solution.py:338
  23.7 0.0 copy-start.8
  23.8 0.0 copy-start.5
  23.8 0.4 collective-permute-start
  24.2 0.0 copy-done
  24.2 0.0 copy-done.2
  24.2 0.4 shard_map.147.part
  24.5 4.0 %collective-permute-done.peer = f32[24,512]{1,0:T(8,128)S(1)} collective-permute-done((f32[24,512]{1,0:T(8,128)S(1)}, f32[24,512]{1,0:T(8,128)S(1)}, u32[]{:S(2)}, u32[]{:S(2)}) %collective-permute-start) | collective-permute-done | bytes 49184 | tf_op jit(solution)/shard_map/ppermute | solution.py:350
  28.6 0.0 collective-permute-done.1.peer
  28.6 1.2 %collective-permute-start.2 = (f32[128,2048]{1,0:T(8,128)S(1)}, f32[128,2048]{1,0:T(8,128)S(1)}, u32[]{:S(2)}, u32[]{:S(2)}) collective-permute-start(f32[128,2048]{1,0:T(8,128)S(1)} %shard_map.147.part), channel_id=1, source_target_pairs={{0,64},{64,0},{1,65},{65,1},{2,66},{66,2},{3,67},{67,3},{4,68},{68... | collective-permute-start | bytes 3145736 | tf_op jit(solution)/shard_map/ppermute | solution.py:352
  29.7 0.0 copy-done.8
  29.7 17.6 %shard_map.148 = (f32[8,64,512]{2,1,0:T(8,128)S(1)}, f32[2,64]{1,0:T(2,128)S(1)}, f32[1,64]{1,0:T(1,128)S(1)}) custom-call(f32[24,512]{1,0:T(8,128)S(1)} %shard_map.146.own, f32[24,512]{1,0:T(8,128)S(1)} %collective-permute-done.peer, f32[2,64]{1,0:T(2,128)S(1)} %copy-done.8), custom_call_target="tpu_custom_call" | custom-call | bytes 52500000 | tf_op jit(solution)/shard_map/pallas_call | solution.py:353
  47.3 0.0 copy-done.5
  47.3 0.0 copy-start.4
  47.3 2.4 %shard_map.149 = (f32[256,2048]{1,0:T(8,128)}, f32[128,2048]{1,0:T(8,128)}, f32[128,2048]{1,0:T(8,128)S(1)}) custom-call(f32[256,2048]{1,0:T(8,128)S(1)} %copy-done.5, f32[128,2048]{1,0:T(8,128)S(1)} %copy-done.2, f32[128,2048]{1,0:T(8,128)S(1)} %shard_map.145.raw, f32[128,2048]{1,0:T(8,128)S(1)} %collective-permute-done.1.peer, ...), custom_call_target="tpu_custom_call" | custom-call | bytes 14000000 | tf_op jit(solution)/shard_map/pallas_call | solution.py:370
  49.8 4.0 %shard_map.151 = (f32[4096,128]{1,0:T(8,128)}, f32[4096,128]{1,0:T(8,128)}, f32[2,64]{1,0:T(2,128)}, f32[1,64]{1,0:T(1,128)}) custom-call(f32[4096,128]{1,0:T(8,128)S(1)} %copy-done.1, f32[4096,128]{1,0:T(8,128)S(1)} %copy-done.4, f32[64,128]{1,0:T(8,128)S(1)} %copy-done.6, f32[8,64,512]{2,1,0:T(8,128)S(1)} %get-tuple-element.22.whole, ...), custom_call_target="tpu_custom_call" | custom-call | bytes 17500000 | tf_op jit(solution)/shard_map/pallas_call | solution.py:361
  53.8 0.0 collective-permute-done.2.peer
  53.8 1.1 %shard_map.150 = f32[256,2048]{1,0:T(8,128)} custom-call(f32[256,2048]{1,0:T(8,128)} %get-tuple-element.25.given, f32[128,2048]{1,0:T(8,128)S(1)} %get-tuple-element.26.base, f32[128,2048]{1,0:T(8,128)S(1)} %collective-permute-done.2.peer), custom_call_target="tpu_custom_call", output_to_operand_aliasing={{}: (0, {})} | custom-call | bytes 3500000 | tf_op jit(solution)/shard_map/pallas_call | solution.py:378
  (1 shorter events, 0.0 us)
Async XLA Ops:
  0.6 4.0 %copy-start.1 = (f32[4096,128]{1,0:T(8,128)S(1)}, f32[4096,128]{1,0:T(8,128)}, u32[]{:S(2)}) copy-start(f32[4096,128]{1,0:T(8,128)} %gate_anchor.3) | copy-start | bytes 6291460
  0.6 4.0 %copy-start.6 = (f32[64,128]{1,0:T(8,128)S(1)}, f32[64,128]{1,0:T(8,128)}, u32[]{:S(2)}) copy-start(f32[64,128]{1,0:T(8,128)} %factor_basis.3) | copy-start | bytes 98308
  0.7 4.0 %copy-start.7 = (f32[1,2,64]{2,1,0:T(2,128)S(1)}, f32[1,2,64]{2,1,0:T(2,128)}, u32[]{:S(2)}) copy-start(f32[1,2,64]{2,1,0:T(2,128)} %norm_local.1) | copy-start | bytes 1540
  0.7 4.0 %copy-start.9 = (f32[1,64]{1,0:T(1,128)S(1)}, f32[1,64]{1,0:T(1,128)}, u32[]{:S(2)}) copy-start(f32[1,64]{1,0:T(1,128)} %norm_moment.1) | copy-start | bytes 772
  2.1 22.1 %copy-start = (f32[1,256,2048]{2,1,0:T(8,128)S(1)}, f32[1,256,2048]{2,1,0:T(8,128)}, u32[]{:S(2)}) copy-start(f32[1,256,2048]{2,1,0:T(8,128)} %down_local.5) | copy-start | bytes 6291460
  2.1 22.1 %copy-start.2 = (f32[128,2048]{1,0:T(8,128)S(1)}, f32[128,2048]{1,0:T(8,128)}, u32[]{:S(2)}) copy-start(f32[128,2048]{1,0:T(8,128)} %down_moment.3) | copy-start | bytes 3145732
  2.1 26.5 %collective-permute-start.1 = (f32[128,2048]{1,0:T(8,128)S(1)}, f32[128,2048]{1,0:T(8,128)S(1)}, u32[]{:S(2)}, u32[]{:S(2)}) collective-permute-start(f32[128,2048]{1,0:T(8,128)S(1)} %shard_map.145.raw), channel_id=1, source_target_pairs={{0,64},{64,0},{1,65},{65,1},{2,66},{66,2},{3,67},{67,3},{4,68},{68... | collective-permute-start | bytes 3145736 | tf_op jit(solution)/shard_map/ppermute | solution.py:333
  4.7 1.6 %copy-start.3 = (f32[1,4096,128]{2,1,0:T(8,128)S(1)}, f32[1,4096,128]{2,1,0:T(8,128)}, u32[]{:S(2)}) copy-start(f32[1,4096,128]{2,1,0:T(8,128)} %gate_local.1) | copy-start | bytes 6291460
  23.7 6.0 %copy-start.8 = (f32[2,64]{1,0:T(2,128)S(1)}, f32[2,64]{1,0:T(2,128)}, u32[]{:S(2)}) copy-start(f32[2,64]{1,0:T(2,128)} %norm_anchor.1) | copy-start | bytes 1540
  23.8 23.6 %copy-start.5 = (f32[256,2048]{1,0:T(8,128)S(1)}, f32[256,2048]{1,0:T(8,128)}, u32[]{:S(2)}) copy-start(f32[256,2048]{1,0:T(8,128)} %down_anchor.1) | copy-start | bytes 6291460
  23.8 4.8 %collective-permute-start = (f32[24,512]{1,0:T(8,128)S(1)}, f32[24,512]{1,0:T(8,128)S(1)}, u32[]{:S(2)}, u32[]{:S(2)}) collective-permute-start(f32[24,512]{1,0:T(8,128)S(1)} %shard_map.146.own), channel_id=1, source_target_pairs={{0,64},{64,0},{1,65},{65,1},{2,66},{66,2},{3,67},{67,3},{4,68},{68... | collective-permute-start | bytes 147464 | tf_op jit(solution)/shard_map/ppermute | solution.py:350
  28.6 25.2 %collective-permute-start.2 = (f32[128,2048]{1,0:T(8,128)S(1)}, f32[128,2048]{1,0:T(8,128)S(1)}, u32[]{:S(2)}, u32[]{:S(2)}) collective-permute-start(f32[128,2048]{1,0:T(8,128)S(1)} %shard_map.147.part), channel_id=1, source_target_pairs={{0,64},{64,0},{1,65},{65,1},{2,66},{66,2},{3,67},{67,3},{4,68},{68... | collective-permute-start | bytes 3145736 | tf_op jit(solution)/shard_map/ppermute | solution.py:352
  47.3 2.5 %copy-start.4 = (f32[4096,128]{1,0:T(8,128)S(1)}, f32[4096,128]{1,0:T(8,128)}, u32[]{:S(2)}) copy-start(f32[4096,128]{1,0:T(8,128)} %gate_moment.1) | copy-start | bytes 6291460
